TPU v7x, 128 devices: a whole 4x4x4 slice. The times are simulated.
128 devices in a mesh: layer: 8 (over x, z_lo), tok: 16 (over y, z_hi, core).
Axes of the slice: x: 4, y: 4, z: 4 (z_hi: 2, z_lo: 2; z = z_hi * 2 + z_lo), core: 2. Of those that a mesh axis runs over, the one named last changes fastest.
Arguments:
- layer_inputs: bfloat16 [8, 512, 2048], P('layer', 'tok'), may hold values from -6 to 6
- layer_targets: bfloat16 [8, 512, 2048], P('layer', 'tok'), may hold values from -12 to 12
- row_order: int32 [512], replicated, may hold values from 0 to 511, each once
- encoder_weight: bfloat16 [8, 2048, 4096], P('layer', None, 'tok'), may hold values from -0.125 to 0.125
- encoder_bias: float32 [8, 4096], P('layer', 'tok'), may hold values from -3 to 3
- decoder_weight: bfloat16 [8, 8, 4096, 2048], P('layer', None, 'tok'), may hold values from -1 to 1
- decoder_bias: float32 [8, 2048], P('layer'), may hold values from -0.6 to 0.6
Outputs:
- encoder_grad: bfloat16 [8, 2048, 4096], P('layer', None, 'tok')
- feature_grad: float32 [8, 4096], P('layer', 'tok')
- decoder_grad: bfloat16 [8, 8, 4096, 2048], P('layer', None, 'tok')
- output_grad: float32 [8, 2048], P('layer')
Inputs may be any that keep to these rules, and one draw needn't show every extreme that they name: Row i of layer_targets belongs to the token in row row_order[i] of layer_inputs, in every layer; each row index appears once.
All inputs are finite; a program needn't handle non-finite values.
Results may differ from a plain program's by a relative error of at most 0.015.
Values may be sent and summed in bfloat16 or wider, within the bound.
A program may use at most 128 MiB of HBM per device.

v0:
```python
import math

import jax
import jax.numpy as jnp
from jax import lax
from jax.sharding import PartitionSpec as P


def on_device(
    layer_inputs,
    layer_targets,
    row_order,
    encoder_weight,
    encoder_bias,
    decoder_weight,
    decoder_bias,
):
    layers = decoder_weight.shape[1]
    row_total = row_order.shape[0]
    loss_scale = 1.0 / math.sqrt(row_total)
    target = lax.axis_index("layer")
    weights = decoder_weight[0]
    width = weights.shape[2]
    features = weights.shape[1]
    contract_rows = (((0,), (0,)), ((), ()))
    contract_cols = (((1,), (1,)), ((), ()))
    squares = jnp.sum(jnp.square(weights.astype(jnp.float32)), axis=2)
    active = (jnp.arange(layers) <= target)[:, None]
    norm_sq = lax.psum(jnp.where(active, squares, 0.0), "layer")
    feature_norms = jnp.sqrt(norm_sq + 1e-06)
    gathered = lax.all_gather(layer_inputs[0], "tok", axis=0, tiled=True)
    ordered = jnp.take(gathered, row_order, axis=0)
    pre_act = (
        jnp.dot(ordered, encoder_weight[0], preferred_element_type=jnp.float32) + encoder_bias[0]
    )
    own_acts = jnp.maximum(pre_act, 0.0).astype(jnp.bfloat16)
    sources = lax.all_gather(own_acts[None], "layer", axis=0, tiled=True)

    def add_source(source, partial_value):
        act_block = lax.dynamic_index_in_dim(sources, source, 0, keepdims=False)
        chosen_weights = lax.dynamic_index_in_dim(weights, source, 0, keepdims=False)
        return partial_value + jnp.dot(
            act_block, chosen_weights, preferred_element_type=jnp.float32
        )

    decoded = lax.psum(
        lax.fori_loop(0, target + 1, add_source, jnp.zeros((row_total, width), jnp.float32)), "tok"
    )
    targets = lax.all_gather(layer_targets[0], "tok", axis=0, tiled=True)
    resid_full = (decoded + decoder_bias[0] - targets.astype(jnp.float32)) * loss_scale
    bias_grad = jnp.sum(resid_full, axis=0)
    residual = resid_full.astype(jnp.bfloat16)

    def source_term(source):

        def source_compute():
            chosen_weights = lax.dynamic_index_in_dim(weights, source, 0, keepdims=False)
            return lax.dot_general(
                residual, chosen_weights, contract_cols, preferred_element_type=jnp.float32
            )

        def source_nothing():
            return jnp.zeros((row_total, features), jnp.float32)

        return lax.cond(source <= target, source_compute, source_nothing)

    grad_acts = lax.psum_scatter(
        lax.map(source_term, jnp.arange(1 * lax.axis_size("layer"), dtype=jnp.int32)),
        "layer",
        scatter_dimension=0,
        tiled=True,
    )[0]
    own_norm = lax.dynamic_index_in_dim(feature_norms, target, 0, keepdims=False)
    grad_pre = jnp.where(pre_act > 0, grad_acts + own_norm * loss_scale, 0.0)
    grad_low = grad_pre.astype(jnp.bfloat16)
    encoder_grad = lax.dot_general(
        ordered, grad_low, contract_rows, preferred_element_type=jnp.float32
    ).astype(jnp.bfloat16)
    feature_grad = jnp.sum(grad_pre, axis=0)
    act_sums = jnp.sum(sources.astype(jnp.float32), axis=1)

    def block_grad(source):

        def block_compute():
            chosen_acts = lax.dynamic_index_in_dim(sources, source, 0, keepdims=False)
            chosen_weights = lax.dynamic_index_in_dim(weights, source, 0, keepdims=False)
            chosen_sums = lax.dynamic_index_in_dim(act_sums, source, 0, keepdims=False)
            chosen_norms = lax.dynamic_index_in_dim(feature_norms, source, 0, keepdims=False)
            factor = chosen_sums * loss_scale / chosen_norms
            product = lax.dot_general(
                chosen_acts, residual, contract_rows, preferred_element_type=jnp.float32
            )
            return (product + factor[:, None] * chosen_weights.astype(jnp.float32)).astype(
                jnp.bfloat16
            )

        def block_nothing():
            return jnp.zeros((features, width), jnp.bfloat16)

        return lax.cond(source <= target, block_compute, block_nothing)

    decoder_grad = lax.map(block_grad, jnp.arange(layers, dtype=jnp.int32))
    return (encoder_grad[None], feature_grad[None], decoder_grad[None], bias_grad[None])


def solution(mesh):
    placed = (
        P("layer", "tok", None),
        P("layer", "tok", None),
        P(),
        P("layer", None, "tok"),
        P("layer", "tok"),
        P("layer", None, "tok", None),
        P("layer", None),
    )
    return jax.shard_map(
        on_device,
        mesh=mesh,
        in_specs=placed,
        out_specs=(
            P("layer", None, "tok"),
            P("layer", "tok"),
            P("layer", None, "tok", None),
            P("layer", None),
        ),
        check_vma=False,
    )
```

profile of v0, /device:TPU:1, one launch (start us, length us, event | category | flops | bytes accessed | tf_op | source)
XLA Modules:
  0.0 489.1 jit_solution(16017502016678263366)
XLA Ops:
  9.3 52.9 %all-gather.7.cloned.1.call-done = bf16[1,512,2048]{2,1,0:T(8,128)(2,1)} async-done(((bf16[1,32,2048]{2,1,0:T(8,128)(2,1)}), bf16[1,512,2048]{2,1,0:T(8,128)(2,1)}) %all-gather.7.cloned.1.call-update) | async-done | bytes 2097168 | tf_op jit(solution)/shard_map/all_gather | solution.py:31
  62.2 6.3 %gather_fusion = bf16[512,2048]{1,0:T(8,128)(2,1)S(1)} fusion(bf16[512,2048]{1,0:T(8,128)(2,1)} %bitcast.65, s32[1024]{0:T(1024)S(1)} %pad_clamp_fusion), kind=kCustom, calls=%fused_computation | custom fusion | bytes 4196352 | tf_op jit(solution)/shard_map/jit(_take)/gather | solution.py:32
  68.6 1.7 maximum_convert_fusion
  71.0 47.3 %all-gather.9.cloned.1.call-done = bf16[4096,256]{1,0:T(8,128)(2,1)} async-done(((bf16[512,256]{1,0:T(8,128)(2,1)}), bf16[4096,256]{1,0:T(8,128)(2,1)}) %all-gather.9.cloned.1.call-update) | async-done | bytes 2097168 | tf_op jit(solution)/shard_map/all_gather | solution.py:37
  118.3 2.5 broadcast_in_dim.73
  120.9 5.3 %while.30 = (s32[]{:T(128)}, f32[512,2048]{1,0:T(8,128)}, s32[]{:T(128)}, bf16[8,512,256]{2,1,0:T(8,128)(2,1)}, bf16[8,256,2048]{2,1,0:T(8,128)(2,1)}, /*index=5*/s32[]{:T(128)}, s32[]{:T(128)}, s32[]{:T(128)}) while((s32[]{:T(128)}, f32[512,2048]{1,0:T(8,128)}, s32[]{:T(128)}, bf16[8,512,256]{2,1,0:T(8,128)(2,1)}, ...), condition=%wide.region_1.2_spmd, body=%wide.region_0.0_spmd.sunk | while | flops 537919488 | bytes 9700471 | solution.py:47
  120.9 5.3 %convolution_add_fusion.4 = f32[512,2048]{1,0:T(8,128)} fusion(f32[512,2048]{1,0:T(8,128)} %get-tuple-element.326, bf16[8,256,2048]{2,1,0:T(8,128)(2,1)} %get-tuple-element.337, s32[]{:T(128)S(6)} %select_n.59, bf16[8,512,256]{2,1,0:T(8,128)(2,1)} %get-tuple-element.336), kind=kOutput, calls=%fused_computation.1.clone.1 | convolution fusion | flops 537919488 | bytes 9700352 | tf_op jit(solution)/shard_map/while/body/dot_general | solution.py:42
  126.3 45.9 %all-gather.11.cloned.1.call-done = bf16[1,512,2048]{2,1,0:T(8,128)(2,1)} async-done(((bf16[1,32,2048]{2,1,0:T(8,128)(2,1)}), bf16[1,512,2048]{2,1,0:T(8,128)(2,1)}) %all-gather.11.cloned.1.call-update) | async-done | bytes 2097168 | tf_op jit(solution)/shard_map/all_gather | solution.py:49
  172.2 152.6 %all-reduce.2.cloned.1.call-done = f32[512,2048]{1,0:T(8,128)} async-done(((f32[512,2048]{1,0:T(8,128)}), f32[512,2048]{1,0:T(8,128)}) %all-reduce.2.cloned.1.call-update) | async-done | bytes 4194320 | tf_op jit(solution)/shard_map/psum | solution.py:46
  324.8 5.7 %fusion.15 = (f32[2048]{0:T(1024)}, bf16[512,2048]{1,0:T(8,128)(2,1)}) fusion(f32[512,2048]{1,0:T(8,128)} %all-reduce.2.cloned.1.call-done, bf16[1,512,2048]{2,1,0:T(8,128)(2,1)} %all-gather.11.cloned.1.call-done, f32[2048]{0:T(1024)S(1)} %bitcast.69), kind=kLoop, calls=%fused_computation.27 | loop fusion | flops 6289408 | bytes 8404992 | tf_op jit(solution)/shard_map/reduce_sum | solution.py:51
  330.5 23.4 %while.31 = (s32[]{:T(128)}, f32[8,512,256]{2,1,0:T(8,128)}, s32[8]{0:T(128)S(1)}, s32[]{:T(128)}, bf16[8,256,2048]{2,1,0:T(8,128)(2,1)}, /*index=5*/bf16[512,2048]{1,0:T(8,128)(2,1)}, s32[]{:T(128)}) while((s32[]{:T(128)}, f32[8,512,256]{2,1,0:T(8,128)}, s32[8]{0:T(128)S(1)}, s32[]{:T(128)}, bf16[8,256,2048]{2,1,0:T(8,128)(2,1)}, ...), condition=%wide.region_6.7_spmd, body=%wide.region_3.6_spmd.sunk | while | flops 536870912 | bytes 5767853 | solution.py:68
  331.8 4.6 conditional.4
  333.7 2.7 convolution_bitcast_fusion
  354.0 5.1 %multiply_reduce_fusion = f32[8,256]{1,0:T(8,128)S(1)} fusion(bf16[1,8,256,2048]{3,2,1,0:T(8,128)(2,1)} %bitcast.67), kind=kLoop, calls=%fused_computation.21 | loop fusion | flops 12580864 | bytes 8396800 | tf_op jit(solution)/shard_map/reduce_sum | solution.py:27
  359.1 53.0 %psum.15 = f32[8,256]{1,0:T(8,128)S(1)} all-reduce(f32[8,256]{1,0:T(8,128)S(1)} %broadcast_select_fusion.3), channel_id=1, replica_groups=mesh['layer'=8,'tok'=16] {'layer'}, use_global_device_ids=true, to_apply=%region_9.10 | all-reduce | flops 2048 | bytes 16384 | tf_op jit(solution)/shard_map/psum | solution.py:29
  412.2 1.9 convert_reduce_fusion
  414.1 25.0 %while.32 = (s32[]{:T(128)}, bf16[8,256,2048]{2,1,0:T(8,128)(2,1)}, s32[8]{0:T(128)S(1)}, s32[]{:T(128)}, bf16[8,512,256]{2,1,0:T(8,128)(2,1)}, /*index=5*/bf16[...) while((s32[]{:T(128)}, bf16[8,256,2048]{2,1,0:T(8,128)(2,1)}, ...), condition=%wide.region_15.16_spmd, body=%wide.region_12.15_spmd.sunk | while | flops 538968576 | bytes 6559453 | solution.py:102
  415.5 4.8 conditional.5
  417.6 2.7 fusion.9
  420.3 1.0 constant_dynamic-update-slice_fusion.5
  422.9 1.0 constant_dynamic-update-slice_fusion.5
  427.9 1.0 constant_dynamic-update-slice_fusion.5
  439.1 39.1 %reduce-scatter.2.cloned.1.call-done = f32[1,512,256]{2,1,0:T(8,128)} async-done(((f32[8,512,256]{2,1,0:T(8,128)}), f32[1,512,256]{2,1,0:T(8,128)}) %reduce-scatter.2.cloned.1.call-update) | async-done | bytes 524304 | tf_op jit(solution)/shard_map/reduce_scatter | solution.py:67
  478.2 3.7 fusion.14
  (100 shorter events, 29.8 us)
Async XLA Ops:
  7.2 61.4 %copy-start = (bf16[1,2048,256]{2,1,0:T(8,128)(2,1)S(1)}, bf16[1,2048,256]{2,1,0:T(8,128)(2,1)}, u32[]{:S(2)}) copy-start(bf16[1,2048,256]{2,1,0:T(8,128)(2,1)} %param.20) | copy-start | bytes 3145732
  7.2 55.1 %all-gather.7.cloned.1.call-start = ((), (), s32[]{:S(2)}) async-start(), calls=%async_computation.3 | async-start | bytes 2228224 | tf_op jit(solution)/shard_map/all_gather | solution.py:31
  7.9 110.4 %all-gather.9.cloned.1.call-start = ((), (), s32[]{:S(2)}) async-start(), calls=%async_computation.4 | async-start | bytes 2359296 | tf_op jit(solution)/shard_map/all_gather | solution.py:37
  62.2 6.3 %copy-start.5 = (f32[1,256]{1,0:T(1,128)S(1)}, f32[1,256]{1,0:T(1,128)}, u32[]{:S(2)}) copy-start(f32[1,256]{1,0:T(1,128)} %param.21) | copy-start | bytes 3076
  68.5 52.3 %copy-start.1 = (bf16[512,2048]{1,0:T(8,128)(2,1)}, bf16[512,2048]{1,0:T(8,128)(2,1)S(1)}, u32[]{:S(2)}) copy-start(bf16[512,2048]{1,0:T(8,128)(2,1)S(1)} %gather_fusion) | copy-start | bytes 6291460
  70.3 101.9 %all-gather.11.cloned.1.call-start = ((), (), s32[]{:S(2)}) async-start(), calls=%async_computation.5 | async-start | bytes 2228224 | tf_op jit(solution)/shard_map/all_gather | solution.py:49
  71.0 253.8 %all-reduce.2.cloned.1.call-start = ((), (), s32[]{:S(2)}) async-start(), calls=%async_computation.1 | async-start | bytes 8388608 | tf_op jit(solution)/shard_map/psum | solution.py:46
  126.2 198.6 %copy-start.4 = (f32[1,2048]{1,0:T(1,128)S(1)}, f32[1,2048]{1,0:T(1,128)}, u32[]{:S(2)}) copy-start(f32[1,2048]{1,0:T(1,128)} %param.23) | copy-start | bytes 24580
  126.2 352.0 %reduce-scatter.2.cloned.1.call-start = ((), (), s32[]{:S(2)}) async-start(), calls=%async_computation.2 | async-start | bytes 4718592 | tf_op jit(solution)/shard_map/reduce_scatter | solution.py:67
  414.1 64.1 %copy-start.2 = (f32[512,256]{1,0:T(8,128)S(1)}, f32[512,256]{1,0:T(8,128)}, u32[]{:S(2)}) copy-start(f32[512,256]{1,0:T(8,128)} %get-tuple-element.192) | copy-start | bytes 1572868
  478.2 3.7 copy-start.3
Sparse Core Ops, SparseCore 0:
  10.4 51.8 all-gather.6
  70.4 47.9 all-gather.8
  120.7 51.4 all-gather.10
  175.2 149.6 all-reduce.1
  354.1 124.0 reduce-scatter.1
where the time goes:
time: 490 us; the launch traced here: 489 us
  waiting for transfers between devices  339 us (69%)
  blocking collectives  53 us (11%)
  local copies, waits for them, and re-layouts  36.5 us (7%)
  matrix products  16 us (3%)
  loops' own time  15.4 us (3%)
  other arithmetic  14.8 us (3%)
  between operations  13.9 us (3%)
    psum x1, waiting for transfers between devices, on_device(): lax.psum(lax.fori_loop(0, target + 1, add_source, jnp.zeros((row_total, w...  153 us
    psum x1, blocking collectives, on_device(): norm_sq = lax.psum(jnp.where(active, squares, 0.0), 'layer')  53 us
    all_gather x1, waiting for transfers between devices, on_device(): gathered = lax.all_gather(layer_inputs[0], 'tok', axis=0, tiled=True)  52.9 us
    all_gather x1, waiting for transfers between devices, on_device(): sources = lax.all_gather(own_acts[None], 'layer', axis=0, tiled=True)  47.3 us
    all_gather x1, waiting for transfers between devices, on_device(): targets = lax.all_gather(layer_targets[0], 'tok', axis=0, tiled=True)  45.9 us
    reduce_scatter x1, waiting for transfers between devices, on_device(): lax.psum_scatter(lax.map(source_term, jnp.arange(1 * lax.axis_size('layer...  39.1 us
    dynamic_slice x16, local copies, waits for them, and re-layouts, on_device(): lax.map(source_term, jnp.arange(1 * lax.axis_size('layer'), dtype=jnp.int...  9.94 us
  transfers between devices with their start and end apart: 5, of which 5 were waited for; matrix products, arithmetic and copies ran while one was open for 7% of the time, Pallas kernels for 0%

commit v1 on v0

v1 whole, which is shorter than its diff:
```python
import math

import jax
import jax.numpy as jnp
from jax import lax
from jax.experimental import pallas as pl
from jax.experimental.pallas import tpu as pltpu
from jax.sharding import PartitionSpec as P

MESH = pl.DeviceIdType.MESH
F32, BF16 = jnp.float32, jnp.bfloat16
NT_DIMS = (((1,), (1,)), ((), ()))
TN_DIMS = (((0,), (0,)), ((), ()))

LAYERS = 8
TOKS = 16
ROWS = 512
D = 2048
FS = 256
CH = 2
PR = 16
CR = TOKS * PR
NT = 512
NSTEPS = D // NT
SCALE = 1.0 / math.sqrt(ROWS)


def main_kernel(
    x_hbm, t_hbm, order_ref, we_hbm, eb_ref, w_hbm, db_ref,
    xo_hbm, ao_hbm, ro_hbm, go_hbm, no_ref,
    xbuf, tbuf, rbuf, acts, pact, bact, pre, we, w,
    opart, sibs, sibr, ys, yr, zs, zr, dkeep,
    gb, gown, frecv, fzs, fzr, gtot, nrecv, gl,
    lsem, osem, ag_s, ag_r, b_s, b_r, cs_s, cs_r, cy_s, cy_r, cz_s, cz_r,
    f_s, f_r, fz_s, fz_r, n_s, n_r,
):
    m, t = lax.axis_index("layer"), lax.axis_index("tok")
    x, zl = m // 2, m % 2
    y, zh, c = t // 4, (t // 2) % 2, t % 2
    yp, ym, yo = (y + 1) % 4, (y + 3) % 4, (y + 2) % 4
    xp, xm = (x + 1) % 4, (x + 3) % 4

    def tk(yy, zz, cc):
        return 4 * yy + 2 * zz + cc

    def by_core(yy, zz, cc):
        return 8 * cc + 2 * yy + zz

    sib, zpt = (m, tk(y, zh, 1 - c)), (m, tk(y, 1 - zh, c))
    yup, ydn = (m, tk(yp, zh, c)), (m, tk(ym, zh, c))
    xup, xdn = (2 * xp + zl, t), (2 * xm + zl, t)
    mp = m + 1 - 2 * zl
    zpl = (mp, t)

    def remote(src, dst, s, r, dev):
        return pltpu.make_async_remote_copy(
            src_ref=src, dst_ref=dst, send_sem=s, recv_sem=r, device_id=dev, device_id_type=MESH
        )

    acts[...] = jnp.zeros_like(acts)

    local = []

    def fetch(src, dst, k):
        cp = pltpu.make_async_copy(src, dst, lsem.at[k])
        cp.start()
        local.append(cp)

    own_core = by_core(y, zh, c)
    for r in range(CH):
        fetch(x_hbm.at[0, pl.ds(r * PR, PR)], xbuf.at[r, own_core], r)
    fetch(we_hbm.at[0], we, 2)
    fetch(t_hbm.at[0], tbuf.at[t], 3)
    for l in range(LAYERS):
        fetch(w_hbm.at[0, l], w.at[pl.ds(l * FS, FS)], 4 + l)

    barrier = pltpu.get_barrier_semaphore()
    for dev in (sib, zpt, yup, ydn):
        pl.semaphore_signal(barrier, inc=1, device_id=dev, device_id_type=MESH)
    for k in range(1, LAYERS):
        pl.semaphore_signal(barrier, inc=1, device_id=((m + k) % LAYERS, t), device_id_type=MESH)
    pl.semaphore_wait(barrier, 4 + LAYERS - 1)

    sent = []

    class Gather:
        def __init__(self, inst, at, own_src, slot):
            self.inst, self.at, self.own_src, self.slot, self.k = inst, at, own_src, slot, 0

        def send(self, src, slot, dev):
            cp = remote(src, self.at(slot), ag_s.at[self.inst, self.k], ag_r.at[self.inst, slot], dev)
            cp.start()
            sent.append(cp)
            self.k += 1

        def wait(self, slot):
            remote(self.at(slot), self.at(slot), ag_s.at[self.inst, 0], ag_r.at[self.inst, slot], sib).wait_recv()

        def pass_on(self, slot, *devs):
            self.wait(slot)
            for dev in devs:
                self.send(self.at(slot), slot, dev)

        def start(self):
            own = self.slot(y, zh, c)
            for dev in (zpt, yup, ydn, sib):
                self.send(self.own_src, own, dev)

        def relay1(self):
            self.pass_on(self.slot(y, 1 - zh, c), yup, ydn, sib)

        def relay2(self):
            self.pass_on(self.slot(ym, zh, c), yup, sib)
            self.pass_on(self.slot(yp, 1 - zh, c), ydn, sib)
            self.pass_on(self.slot(yp, zh, c), sib)
            self.pass_on(self.slot(ym, 1 - zh, c), sib)

        def finish(self):
            self.pass_on(self.slot(yo, zh, c), sib)
            self.pass_on(self.slot(yo, 1 - zh, c), sib)
            for yy in range(4):
                for zz in range(2):
                    self.wait(self.slot(yy, zz, 1 - c))

    ax = [
        Gather(r, (lambda s, r=r: xbuf.at[r, s]), x_hbm.at[0, pl.ds(r * PR, PR)], by_core)
        for r in range(CH)
    ]
    at = Gather(2, (lambda s: tbuf.at[s]), t_hbm.at[0], tk)
    ar = [
        Gather(3 + r, (lambda s, r=r: rbuf.at[r, s]), rbuf.at[r, own_core], by_core)
        for r in range(CH)
    ]

    outs = []

    def put(src, dst, k):
        cp = pltpu.make_async_copy(src, dst, osem.at[k])
        cp.start()
        outs.append(cp)

    def encode(r):
        rows = xbuf[r].reshape(CR, D)
        value = jnp.dot(rows, we[...], preferred_element_type=F32) + eb_ref[...]
        pre[r] = value
        acts[r, :, pl.ds(pl.multiple_of(m * FS, FS), FS)] = jnp.maximum(value, 0.0).astype(BF16)

    def act_at(r, l):
        return acts.at[r, :, pl.ds(pl.multiple_of(l * FS, FS), FS)]

    def b_copy(r, k, src, dst, slot, dev):
        return remote(src, dst, b_s.at[r, k], b_r.at[r, slot], dev)

    def b_wait(r, l):
        b_copy(r, 0, act_at(r, l), act_at(r, l), l, sib).wait_recv()

    def b_own(r):
        return [
            (None, b_copy(r, 0, act_at(r, m), pact.at[r], 8, zpl)),
            (x < 3, b_copy(r, 1, act_at(r, m), act_at(r, m), m, xup)),
            (x == 0, b_copy(r, 2, act_at(r, m), act_at(r, m), m, xdn)),
            (m == 3, b_copy(r, 3, act_at(r, m), bact.at[r], 9, xdn)),
        ]

    def b_partner(r):
        return [
            (x < 3, b_copy(r, 4, pact.at[r], act_at(r, mp), mp, xup)),
            (x == 0, b_copy(r, 5, pact.at[r], act_at(r, mp), mp, xdn)),
            (m == 2, b_copy(r, 6, pact.at[r], bact.at[r], 9, xdn)),
        ]

    def b_relay(r):
        return [
            (x == 0, (9,), [b_copy(r, 7, bact.at[r], act_at(r, 3), 3, xdn)]),
            (x == 2, (2,), [b_copy(r, 7, act_at(r, 2), act_at(r, 2), 2, xup)]),
            (x == 3, (0, 1), [b_copy(r, 7 + l, act_at(r, l), act_at(r, l), l, xdn) for l in (0, 1)]),
        ]

    def when(cond, fn):
        if cond is None:
            fn()
        else:
            pl.when(cond)(fn)

    def b_start(r):
        for cond, cp in b_own(r):
            when(cond, cp.start)

    def b_step1(r):
        remote(pact.at[r], pact.at[r], b_s.at[r, 0], b_r.at[r, 8], sib).wait_recv()
        for cond, cp in b_partner(r):
            when(cond, cp.start)

        @pl.when(zl == 1)
        def _():
            acts[r, :, pl.ds(pl.multiple_of(mp * FS, FS), FS)] = pact[r]

    def b_step2(r):
        for cond, slots, copies in b_relay(r):

            def go(slots=slots, copies=copies):
                for slot, cp in zip(slots, copies):
                    if slot == 9:
                        remote(bact.at[r], bact.at[r], b_s.at[r, 0], b_r.at[r, 9], sib).wait_recv()
                    else:
                        b_wait(r, slot)
                    cp.start()

            when(cond, go)

    def b_finish(r):
        for cond, slots in ((x == 1, (0, 1)), (x == 2, (0, 1, 3)), (x == 3, (2, 3, 4, 5))):
            when(cond, lambda slots=slots: [b_wait(r, l) for l in slots] and None)

    def b_drain(r):
        for cond, cp in b_own(r) + b_partner(r):
            when(cond, cp.wait_send)
        for cond, _, copies in b_relay(r):
            when(cond, lambda copies=copies: [cp.wait_send() for cp in copies] and None)

    def norm_copy(k):
        return remote(nrecv.at[m], nrecv.at[m], n_s.at[k], n_r.at[m], ((m + k) % LAYERS, t))

    def norms():
        for k in range(4, 4 + LAYERS):
            local[k].wait()

        @pl.loop(0, LAYERS)
        def _(l):
            part = jnp.zeros((FS, 128), F32)
            for j in range(D // 128):
                v = w[pl.ds(pl.multiple_of(l * FS, FS), FS), j * 128 : (j + 1) * 128].astype(F32)
                part = part + v * v
            row = lax.dot_general(
                jnp.ones((8, 128), F32), part, NT_DIMS,
                preferred_element_type=F32, precision=lax.Precision.HIGHEST,
            )
            keep = jnp.where(l <= m, 1.0, 0.0).astype(F32)
            nrecv[m, pl.ds(l, 1), :] = row[0:1] * keep

        for k in range(1, LAYERS):
            norm_copy(k).start()

    def norms_finish():
        for k in range(1, LAYERS):
            s = (m + k) % LAYERS
            remote(nrecv.at[s], nrecv.at[s], n_s.at[0], n_r.at[s], sib).wait_recv()
        total = nrecv[0]
        for s in range(1, LAYERS):
            total = total + nrecv[s]
        no_ref[...] = jnp.sqrt(total + 1e-06)

    def decode(r):
        rows = jnp.concatenate(
            [
                acts[r, pl.ds(pl.multiple_of((1 - c) * 128, 128), 128), :],
                acts[r, pl.ds(pl.multiple_of(c * 128, 128), 128), :],
            ],
            axis=0,
        )

        @pl.loop(0, NSTEPS)
        def _(n):
            part = jnp.dot(
                rows, w[:, pl.ds(pl.multiple_of(n * NT, NT), NT)], preferred_element_type=F32
            )
            sibs[r, n] = part[:128].astype(BF16)
            opart[r, n] = part[128:]
            remote(sibs.at[r, n], sibr.at[r, n], cs_s.at[r, n], cs_r.at[r, n], sib).start()

    def chip_sum(r, q, n):
        rows = pl.ds(pl.multiple_of(q * PR, PR), PR)
        return opart[r, n, rows, :] + sibr[r, n, rows, :].astype(F32)

    def cols(n):
        return slice(n * NT, (n + 1) * NT)

    def y_copy(r, k):
        dev = yup if k in (0, 2, 3) else ydn
        return remote(ys.at[r, k], yr.at[r, k], cy_s.at[r, k], cy_r.at[r, k], dev)

    def y_wait(r, k):
        remote(yr.at[r, k], yr.at[r, k], cy_s.at[r, k], cy_r.at[r, k], sib).wait_recv()

    def c_a(r):
        for n in range(NSTEPS):
            remote(sibr.at[r, n], sibr.at[r, n], cs_s.at[r, n], cs_r.at[r, n], sib).wait_recv()
        for k, q in ((0, 2 * yo), (1, 2 * yo + 1), (3, 2 * yp + 1), (4, 2 * ym)):
            for n in range(NSTEPS):
                ys[r, k, :, cols(n)] = chip_sum(r, q, n).astype(BF16)
            y_copy(r, k).start()

    def c_b(r):
        for k, q, i in ((2, 2 * yp, 0), (5, 2 * ym + 1, 1)):
            y_wait(r, i)
            for n in range(NSTEPS):
                ys[r, k, :, cols(n)] = (
                    chip_sum(r, q, n) + yr[r, i, :, cols(n)].astype(F32)
                ).astype(BF16)
            y_copy(r, k).start()

    def z_copy(r):
        return remote(zs.at[r], zr.at[r], cz_s.at[r], cz_r.at[r], zpt)

    def c_c(r):
        for k in (2, 3, 4, 5):
            y_wait(r, k)
        for n in range(NSTEPS):
            other = chip_sum(r, 2 * y + 1 - zh, n)
            other = other + yr[r, 3 - zh, :, cols(n)].astype(F32)
            other = other + yr[r, 5 - zh, :, cols(n)].astype(F32)
            zs[r, :, cols(n)] = other.astype(BF16)
        z_copy(r).start()
        for n in range(NSTEPS):
            mine = chip_sum(r, 2 * y + zh, n)
            mine = mine + yr[r, 2 + zh, :, cols(n)].astype(F32)
            mine = mine + yr[r, 4 + zh, :, cols(n)].astype(F32)
            dkeep[:, cols(n)] = mine

    def c_d(r):
        ids = lax.broadcasted_iota(jnp.int32, (PR, ROWS), 0) + (2 * PR * t + PR * r)
        pick = (jnp.broadcast_to(order_ref[...], (PR, ROWS)) == ids).astype(F32).astype(BF16)
        wanted = jnp.dot(pick, tbuf[...].reshape(ROWS, D), preferred_element_type=F32)
        remote(zr.at[r], zr.at[r], cz_s.at[r], cz_r.at[r], sib).wait_recv()
        resid = (dkeep[...] + zr[r].astype(F32) + db_ref[...] - wanted) * SCALE
        rbuf[r, own_core] = resid.astype(BF16)
        ar[r].start()

    def f_copy(r, k, src, slot, dev):
        return remote(src, frecv.at[r, slot], f_s.at[r, k], f_r.at[r, slot], dev)

    def f_wait(r, slot):
        remote(frecv.at[r, slot], frecv.at[r, slot], f_s.at[r, 0], f_r.at[r, slot], sib).wait_recv()

    def f_sends(r, name):
        return {
            "a1": lambda: [f_copy(r, l, gb.at[r, l], l, xdn) for l in (0, 1)],
            "a2": lambda: [f_copy(r, l, gb.at[r, l], 2 + l, xup) for l in (0, 1)],
            "a3": lambda: [f_copy(r, 3, gb.at[r, 3], 4, xup), f_copy(r, 2, gb.at[r, 2], 4, xdn)],
            "b2": lambda: [f_copy(r, 3, gb.at[r, 3], 1, xdn)],
            "s2": lambda: [f_copy(r, 2, gb.at[r, 2], 0, xdn)],
            "b3": lambda: [f_copy(r, 4 + l, gb.at[r, 4 + l], l, xdn) for l in (0, 1)],
            "c3": lambda: [f_copy(r, l, gb.at[r, l], 2 + l, xup) for l in (0, 1)],
            "r0": lambda: [f_copy(r, 7, frecv.at[r, 4], 2, xup)],
        }[name]()

    def f_go(r, name, before=None):
        @pl.when(x == int(name[1]))
        def _():
            if before is not None:
                before()
            for cp in f_sends(r, name):
                cp.start()

    def grads(r, i):
        @pl.when(i <= x)
        def _():
            p = (i + x // 3) % 3 if i < 3 else 3
            g = lax.dot_general(
                rbuf[r].reshape(CR, D), w[pl.ds(pl.multiple_of(p * 2 * FS, 2 * FS), 2 * FS), :],
                NT_DIMS, preferred_element_type=F32,
            )

            @pl.when(x != i)
            def _():
                gb[r, 2 * p] = g[:, :FS].astype(BF16)
                gb[r, 2 * p + 1] = g[:, FS:].astype(BF16)

            @pl.when(x == i)
            def _():
                gown[r, 0] = g[:, :FS]
                gown[r, 1] = g[:, FS:] * zl.astype(F32)

        def add(pairs):
            def fn():
                for l, slot in pairs:
                    f_wait(r, slot)
                    gb[r, l] = (gb[r, l].astype(F32) + frecv[r, slot].astype(F32)).astype(BF16)

            return fn

        if i == 0:
            for name in ("a1", "a2", "a3"):
                f_go(r, name)
        if i == 1:
            f_go(r, "b2")
            f_go(r, "b3")
            f_go(r, "s2", add(((2, 4),)))
        if i == 2:
            f_go(r, "c3", add(((0, 2), (1, 3))))

    def f_relay(r):
        f_go(r, "r0", lambda: f_wait(r, 4))

    def f_zcopy(r):
        return remote(fzs.at[r], fzr.at[r], fz_s.at[r], fz_r.at[r], zpl)

    def f_fin1(r):
        for cond, adds in (
            (x == 0, ((0, 0), (1, 1), (0, 2), (1, 3))),
            (x == 1, ((0, 0), (1, 1), (1, 2))),
            (x == 2, ((0, 0), (1, 1))),
        ):

            @pl.when(cond)
            def _(adds=adds):
                for j, slot in adds:
                    f_wait(r, slot)
                    gown[r, j] = gown[r, j] + frecv[r, slot].astype(F32)

        fzs[r] = gown[r, 1 - zl].astype(BF16)
        f_zcopy(r).start()

    def f_fin2(r):
        remote(fzr.at[r], fzr.at[r], fz_s.at[r], fz_r.at[r], sib).wait_recv()
        total = gown[r, zl] + fzr[r].astype(F32)
        norm = no_ref[pl.ds(m, 1), :]
        grad = jnp.where(pre[r] > 0, total + norm * SCALE, 0.0)
        gl[r] = grad.astype(BF16)
        put(gl.at[r], go_hbm.at[pl.ds(r * CR, CR)], 6 + r)

    ax[0].start()
    ax[1].start()
    for k in range(3):
        local[k].wait()
    ax[0].relay1()
    ax[1].relay1()
    ax[0].relay2()
    ax[0].finish()
    encode(0)
    b_start(0)
    ax[1].relay2()
    ax[1].finish()
    encode(1)
    b_start(1)
    at.start()
    for r in range(CH):
        put(xbuf.at[r], xo_hbm.at[r], r)
    b_step1(0)
    b_step1(1)
    norms()
    local[3].wait()
    at.relay1()
    b_step2(0)
    b_step2(1)
    at.relay2()
    at.finish()
    b_finish(0)
    decode(0)
    put(acts.at[0], ao_hbm.at[0], 2)
    c_a(0)
    b_finish(1)
    decode(1)
    put(acts.at[1], ao_hbm.at[1], 3)
    c_b(0)
    c_a(1)
    c_c(0)
    c_d(0)
    c_b(1)
    ar[0].relay1()
    c_c(1)
    ar[0].relay2()
    c_d(1)
    norms_finish()
    ar[0].finish()
    put(rbuf.at[0], ro_hbm.at[0], 4)
    grads(0, 0)
    ar[1].relay1()
    grads(0, 1)
    ar[1].relay2()
    grads(0, 2)
    ar[1].finish()
    put(rbuf.at[1], ro_hbm.at[1], 5)
    grads(0, 3)
    f_relay(0)
    grads(1, 0)
    f_relay(1)
    grads(1, 1)
    f_fin1(0)
    grads(1, 2)
    grads(1, 3)
    f_fin2(0)
    f_fin1(1)
    f_fin2(1)

    for cp in sent:
        cp.wait_send()
    for r in range(CH):
        b_drain(r)
        for n in range(NSTEPS):
            remote(sibs.at[r, n], sibr.at[r, n], cs_s.at[r, n], cs_r.at[r, n], sib).wait_send()
        for k in range(6):
            y_copy(r, k).wait_send()
        z_copy(r).wait_send()
        for name in ("a1", "a2", "a3", "b2", "s2", "b3", "c3", "r0"):

            @pl.when(x == int(name[1]))
            def _(name=name):
                for cp in f_sends(r, name):
                    cp.wait_send()

        f_zcopy(r).wait_send()
    for k in range(1, LAYERS):
        norm_copy(k).wait_send()
    for cp in outs:
        cp.wait()


def run_main(x, tgt, order, we, eb, w, db):
    any_spec = pl.BlockSpec(memory_space=pl.ANY)
    vmem = pl.BlockSpec(memory_space=pltpu.VMEM)
    dma = pltpu.SemaphoreType.DMA
    return pl.pallas_call(
        main_kernel,
        out_shape=(
            jax.ShapeDtypeStruct((CH, TOKS, PR, D), BF16),
            jax.ShapeDtypeStruct((CH, CR, D), BF16),
            jax.ShapeDtypeStruct((CH, TOKS, PR, D), BF16),
            jax.ShapeDtypeStruct((CH * CR, FS), BF16),
            jax.ShapeDtypeStruct((LAYERS, FS), F32),
        ),
        in_specs=[any_spec, any_spec, vmem, any_spec, vmem, any_spec, vmem],
        out_specs=(any_spec, any_spec, any_spec, any_spec, vmem),
        scratch_shapes=[
            pltpu.VMEM((CH, TOKS, PR, D), BF16),
            pltpu.VMEM((TOKS, 2 * PR, D), BF16),
            pltpu.VMEM((CH, TOKS, PR, D), BF16),
            pltpu.VMEM((CH, CR, D), BF16),
            pltpu.VMEM((CH, CR, FS), BF16),
            pltpu.VMEM((CH, CR, FS), BF16),
            pltpu.VMEM((CH, CR, FS), F32),
            pltpu.VMEM((D, FS), BF16),
            pltpu.VMEM((LAYERS * FS, D), BF16),
            pltpu.VMEM((CH, NSTEPS, 128, NT), F32),
            pltpu.VMEM((CH, NSTEPS, 128, NT), BF16),
            pltpu.VMEM((CH, NSTEPS, 128, NT), BF16),
            pltpu.VMEM((CH, 6, PR, D), BF16),
            pltpu.VMEM((CH, 6, PR, D), BF16),
            pltpu.VMEM((CH, PR, D), BF16),
            pltpu.VMEM((CH, PR, D), BF16),
            pltpu.VMEM((PR, D), F32),
            pltpu.VMEM((CH, LAYERS, CR, FS), BF16),
            pltpu.VMEM((CH, 2, CR, FS), F32),
            pltpu.VMEM((CH, 5, CR, FS), BF16),
            pltpu.VMEM((CH, CR, FS), BF16),
            pltpu.VMEM((CH, CR, FS), BF16),
            pltpu.VMEM((8, 128), F32),
            pltpu.VMEM((LAYERS, LAYERS, FS), F32),
            pltpu.VMEM((CH, CR, FS), BF16),
            dma((4 + LAYERS,)), dma((8,)), dma((5, 15)), dma((5, TOKS)),
            dma((CH, 9)), dma((CH, 10)), dma((CH, NSTEPS)), dma((CH, NSTEPS)),
            dma((CH, 6)), dma((CH, 6)), dma((CH,)), dma((CH,)),
            dma((CH, 8)), dma((CH, 5)), dma((CH,)), dma((CH,)),
            dma((LAYERS,)), dma((LAYERS,)),
        ],
        compiler_params=pltpu.CompilerParams(
            collective_id=0, has_side_effects=True, vmem_limit_bytes=60 << 20
        ),
        name="window",
    )(x, tgt, order, we, eb, w, db)


def tail_kernel(m_ref, a_ref, r_ref, w_ref, n_ref, x_ref, g_ref, dw_ref, dwe_ref, fg_ref, og_ref):
    l = pl.program_id(0)
    m = m_ref[0]

    @pl.when(l == 0)
    def _():
        ones = jnp.ones((8, ROWS), BF16)
        g = g_ref[...]
        fg_ref[...] = jnp.dot(ones, g, preferred_element_type=F32)[0:1]
        og_ref[...] = jnp.dot(ones, r_ref[...], preferred_element_type=F32)[0:1]
        flipped = jnp.dot(g.T, x_ref[...], preferred_element_type=F32).astype(BF16)
        dwe_ref[...] = flipped.T

    @pl.when(l > m)
    def _():
        dw_ref[...] = jnp.zeros_like(dw_ref)

    @pl.when(l <= m)
    def _():
        at = a_ref[...].T
        sums = jnp.dot(at, jnp.ones((ROWS, 128), BF16), preferred_element_type=F32)
        pick = (lax.broadcasted_iota(jnp.int32, (LAYERS, 128), 0) == l).astype(F32)
        norm = lax.dot_general(
            n_ref[...], pick, TN_DIMS, preferred_element_type=F32, precision=lax.Precision.HIGHEST
        )
        factor = sums * SCALE / norm
        for n in range(4):
            cs = slice(n * 512, (n + 1) * 512)
            prod = jnp.dot(at, r_ref[:, cs], preferred_element_type=F32)
            fac = jnp.concatenate([factor] * 4, axis=1)
            dw_ref[0, :, cs] = (prod + fac * w_ref[0, :, cs].astype(F32)).astype(BF16)


def run_tail(m, acts, resid, w, norms, xs, gl):
    def fixed(shape):
        return pl.BlockSpec(shape, lambda l, m: (0,) * len(shape), pipeline_mode=pl.Buffered(1))

    return pl.pallas_call(
        tail_kernel,
        out_shape=(
            jax.ShapeDtypeStruct((LAYERS, FS, D), BF16),
            jax.ShapeDtypeStruct((D, FS), BF16),
            jax.ShapeDtypeStruct((1, FS), F32),
            jax.ShapeDtypeStruct((1, D), F32),
        ),
        grid_spec=pltpu.PrefetchScalarGridSpec(
            num_scalar_prefetch=1,
            grid=(LAYERS,),
            in_specs=[
                pl.BlockSpec((ROWS, FS), lambda l, m: (0, jnp.minimum(l, m[0]))),
                fixed((ROWS, D)),
                pl.BlockSpec((1, FS, D), lambda l, m: (jnp.minimum(l, m[0]), 0, 0)),
                fixed((LAYERS, FS)),
                fixed((ROWS, D)),
                fixed((ROWS, FS)),
            ],
            out_specs=(
                pl.BlockSpec((1, FS, D), lambda l, m: (l, 0, 0)),
                pl.BlockSpec((D, FS), lambda l, m: (0, 0)),
                pl.BlockSpec((1, FS), lambda l, m: (0, 0)),
                pl.BlockSpec((1, D), lambda l, m: (0, 0)),
            ),
        ),
        compiler_params=pltpu.CompilerParams(vmem_limit_bytes=50 << 20),
        name="weights",
    )(m, acts, resid, w, norms, xs, gl)


def on_device(x, tgt, order, we, eb, w, db):
    xs, acts, resid, gl, norms = run_main(x, tgt, order[None], we, eb, w, db)
    m = lax.axis_index("layer").astype(jnp.int32)[None]
    dw, dwe, fg, og = run_tail(
        m, acts.reshape(ROWS, D), resid.reshape(ROWS, D), w[0], norms, xs.reshape(ROWS, D), gl
    )
    return dwe[None], fg, dw[None], og


def solution(mesh):
    placed = (
        P("layer", "tok", None),
        P("layer", "tok", None),
        P(),
        P("layer", None, "tok"),
        P("layer", "tok"),
        P("layer", None, "tok", None),
        P("layer", None),
    )
    return jax.shard_map(
        on_device,
        mesh=mesh,
        in_specs=placed,
        out_specs=(
            P("layer", None, "tok"),
            P("layer", "tok"),
            P("layer", None, "tok", None),
            P("layer", None),
        ),
        check_vma=False,
    )
```

time: 490 us -> 120 us (0.24)
  waiting for transfers between devices: 339 us -> 0 us
  Pallas kernels: 0 us -> 115 us
  blocking collectives: 53 us -> 0 us
  local copies, waits for them, and re-layouts: 36.5 us -> 3.23 us
  matrix products: 16 us -> 0 us
  loops' own time: 15.4 us -> 0 us
  other arithmetic: 14.8 us -> 0 us
  between operations: 13.9 us -> 0.66 us
    psum x1 -> x0, waiting for transfers between devices: 153 us -> none  [on_device(): lax.psum(lax.fori_loop(0, target + 1, add_source, jnp.zeros((row_total, w...]
    all_gather x3 -> x0, waiting for transfers between devices: 146 us -> none  [the longest x1 52.9 us: on_device(): gathered = lax.all_gather(layer_inputs[0], 'tok', axis=0, tiled=True)]
    pallas_call x0 -> x2, Pallas kernels: none -> 115 us  [the longest x1 105 us: run_main(): pl.pallas_call(main_kernel, out_shape=(jax.ShapeDtypeStruct((CH, TOKS, PR...]
    psum x1 -> x0, blocking collectives: 53 us -> none  [on_device(): norm_sq = lax.psum(jnp.where(active, squares, 0.0), 'layer')]
    reduce_scatter x1 -> x0, waiting for transfers between devices: 39.1 us -> none  [on_device(): lax.psum_scatter(lax.map(source_term, jnp.arange(1 * lax.axis_size('layer...]
    dynamic_update_slice x24 -> x0, local copies, waits for them, and re-layouts: 16.6 us -> none  [the longest x8 8.35 us: on_device(): decoder_grad = lax.map(block_grad, jnp.arange(layers, dtype=jnp.int32))]
    dot_general x5 -> x0, matrix products: 16 us -> none  [the longest x1 5.32 us: add_source(): jnp.dot(act_block, chosen_weights, preferred_element_type=jnp.float32)]
    another operation x19 -> x0, loops' own time: 15.4 us -> none  [the longest x1 5.67 us: on_device(): decoder_grad = lax.map(block_grad, jnp.arange(layers, dtype=jnp.int32))]
  transfers between devices with their start and end apart: 5 -> 0, of which waited for: 5 -> 0; matrix products, arithmetic and copies ran while one was open for 7% -> 0% of each run, Pallas kernels for 0% -> 0%
where the time goes in v1:
time: 120 us; the launch traced here: 119 us
  Pallas kernels  115 us (96%)
  local copies, waits for them, and re-layouts  3.23 us (3%)
    pallas_call x1, Pallas kernels, run_main(): pl.pallas_call(main_kernel, out_shape=(jax.ShapeDtypeStruct((CH, TOKS, PR...  105 us
    pallas_call x1, Pallas kernels, run_tail(): pl.pallas_call(tail_kernel, out_shape=(jax.ShapeDtypeStruct((LAYERS, FS,...  9.41 us
    unnamed x6, local copies, waits for them, and re-layouts  3.23 us

profile of v1, /device:TPU:1, one launch (start us, length us, event | category | flops | bytes accessed | tf_op | source)
XLA Modules:
  0.0 118.7 jit_solution(6167390475952130144)
XLA Ops:
  0.6 105.4 %window.1 = (bf16[2,16,16,2048]{3,2,1,0:T(8,128)(2,1)}, bf16[2,256,2048]{2,1,0:T(8,128)(2,1)}, bf16[2,16,16,2048]{3,2,1,0:T(8,128)(2,1)}, bf16[512,256]{1,0:T(8,128)(2,1)}, f32[8,256]{1,0:T(8,128)}) custom-call(bf16[1,32,2048]{2,1,0:T(8,128)(2,1)} %x_hbm.1, bf16[1,32,2048]{2,1,0:T(8,128)(2,1)} %t_hbm.1, s32[1,512]{1,0:T(1,128)} %bitcast.12, ...), custom_call_target="tpu_custom_call" | custom-call | tf_op jit(solution)/shard_map/window/pallas_call | solution.py:513
  106.1 0.0 copy-start
  106.1 1.6 %copy-done = bf16[2,256,2048]{2,1,0:T(8,128)(2,1)S(1)} copy-done((bf16[2,256,2048]{2,1,0:T(8,128)(2,1)S(1)}, bf16[2,256,2048]{2,1,0:T(8,128)(2,1)}, u32[]{:S(2)}) %copy-start) | copy-done | bytes 2097176
  107.7 0.0 copy-start.1
  107.7 0.9 copy-done.1
  108.6 0.0 copy-start.2
  108.6 0.7 copy-done.2
  109.3 9.4 %weights.1 = (bf16[8,256,2048]{2,1,0:T(8,128)(2,1)}, bf16[2048,256]{1,0:T(8,128)(2,1)}, f32[1,256]{1,0:T(1,128)}, f32[1,2048]{1,0:T(1,128)}) custom-call(s32[1]{0:T(128)} %bitcast.m_ref, bf16[512,2048]{1,0:T(8,128)(2,1)S(1)} %bitcast.8, bf16[512,2048]{1,0:T(8,128)(2,1)} %bitcast.11, bf16[8,256,2048]{2,1,0:T(8,128)(2,1)} %bitcast.9, f32[8,256]{1,0:T(8,128)S(1)} %copy-done.2, ...), custom_call_target="tpu_custom_call" | custom-call | tf_op jit(solution)/shard_map/weights/pallas_call | solution.py:600
Async XLA Ops:
  106.1 1.6 %copy-start = (bf16[2,256,2048]{2,1,0:T(8,128)(2,1)S(1)}, bf16[2,256,2048]{2,1,0:T(8,128)(2,1)}, u32[]{:S(2)}) copy-start(bf16[2,256,2048]{2,1,0:T(8,128)(2,1)} %get-tuple-element.13) | copy-start | bytes 6291460
  107.7 0.9 copy-start.1
  108.6 0.7 copy-start.2

commit v2 on v1

v2 whole, which is shorter than its diff:
```python
import math

import jax
import jax.numpy as jnp
from jax import lax
from jax.experimental import pallas as pl
from jax.experimental.pallas import tpu as pltpu
from jax.sharding import PartitionSpec as P

MESH = pl.DeviceIdType.MESH
F32, BF16 = jnp.float32, jnp.bfloat16
NT_DIMS = (((1,), (1,)), ((), ()))
TN_DIMS = (((0,), (0,)), ((), ()))

LAYERS = 8
TOKS = 16
ROWS = 512
D = 2048
FS = 256
CH = 2
PR = 16
CR = TOKS * PR
NT = 512
NSTEPS = D // NT
HALVES = 2
HW = D // HALVES
HS = NSTEPS // HALVES
SCALE = 1.0 / math.sqrt(ROWS)


def main_kernel(
    x_hbm, t_hbm, order_ref, we_hbm, eb_ref, w_hbm, db_ref,
    xo, go, do, fo, oo,
    tbuf, rbuf, acts, pact, bact, pre, we, w,
    opart, sibs, sibr, ys, yr, zs, zr, dkeep, tpick,
    gb, gown, frecv, fzs, fzr, nrecv, no_ref, act_t,
    lsem, ag_s, ag_r, b_s, b_r, cs_s, cs_r, cy_s, cy_r, cz_s, cz_r,
    f_s, f_r, fz_s, fz_r, n_s, n_r,
):
    m, t = lax.axis_index("layer"), lax.axis_index("tok")
    x, zl = m // 2, m % 2
    y, zh, c = t // 4, (t // 2) % 2, t % 2
    yp, ym, yo = (y + 1) % 4, (y + 3) % 4, (y + 2) % 4
    xp, xm = (x + 1) % 4, (x + 3) % 4

    def tk(yy, zz, cc):
        return 4 * yy + 2 * zz + cc

    def by_core(yy, zz, cc):
        return 8 * cc + 2 * yy + zz

    sib, zpt = (m, tk(y, zh, 1 - c)), (m, tk(y, 1 - zh, c))
    yup, ydn = (m, tk(yp, zh, c)), (m, tk(ym, zh, c))
    xup, xdn = (2 * xp + zl, t), (2 * xm + zl, t)
    mp = m + 1 - 2 * zl
    zpl = (mp, t)

    def remote(src, dst, s, r, dev):
        return pltpu.make_async_remote_copy(
            src_ref=src, dst_ref=dst, send_sem=s, recv_sem=r, device_id=dev, device_id_type=MESH
        )

    local = []

    def fetch(src, dst, k):
        cp = pltpu.make_async_copy(src, dst, lsem.at[k])
        cp.start()
        local.append(cp)

    own_core = by_core(y, zh, c)
    for r in range(CH):
        fetch(x_hbm.at[0, pl.ds(r * PR, PR)], xo.at[r, own_core], r)
    fetch(we_hbm.at[0], we, 2)
    fetch(t_hbm.at[0], tbuf.at[t], 3)
    for l in range(LAYERS):
        fetch(w_hbm.at[0, l], w.at[pl.ds(l * FS, FS)], 4 + l)

    barrier = pltpu.get_barrier_semaphore()
    for dev in (sib, zpt, yup, ydn):
        pl.semaphore_signal(barrier, inc=1, device_id=dev, device_id_type=MESH)
    for k in range(1, LAYERS):
        pl.semaphore_signal(barrier, inc=1, device_id=((m + k) % LAYERS, t), device_id_type=MESH)
    pl.semaphore_wait(barrier, 4 + LAYERS - 1)

    class Gather:
        def __init__(self, inst, at, many, slot):
            self.inst, self.at, self.many, self.slot = inst, at, many, slot

        def send(self, slot, dev, sem):
            remote(self.at(slot), self.at(slot), ag_s.at[self.inst], ag_r.at[self.inst, sem], dev).start()

        def wait(self, slot, sem):
            remote(self.at(slot), self.at(slot), ag_s.at[self.inst], ag_r.at[self.inst, sem], sib).wait_recv()

        def to_sib(self, yy, zz):
            shared = self.slot is by_core
            self.send(self.slot(yy, zz, c), sib, 8 if shared else 8 + 2 * yy + zz)

        def to(self, yy, zz, *devs):
            for dev in devs:
                self.send(self.slot(yy, zz, c), dev, 2 * yy + zz)

        def take(self, yy, zz):
            self.wait(self.slot(yy, zz, c), 2 * yy + zz)

        def start(self):
            self.to(y, zh, zpt, yup, ydn)
            self.to_sib(y, zh)

        def relay_z(self):
            self.take(y, 1 - zh)
            self.to(y, 1 - zh, yup, ydn)
            self.to_sib(y, 1 - zh)

        def relay_y(self):
            self.take(ym, zh)
            self.to(ym, zh, yup)
            self.to_sib(ym, zh)
            self.take(yp, zh)
            self.to_sib(yp, zh)

        def relay_zy(self):
            self.take(yp, 1 - zh)
            self.to(yp, 1 - zh, ydn)
            self.to_sib(yp, 1 - zh)
            self.take(ym, 1 - zh)
            self.to_sib(ym, 1 - zh)

        def far_y(self):
            self.take(yo, zh)
            self.to_sib(yo, zh)

        def finish(self):
            self.take(yo, 1 - zh)
            self.to_sib(yo, 1 - zh)
            if self.slot is by_core:
                ref = self.many(8 * (1 - c), 8)
                remote(ref, ref, ag_s.at[self.inst], ag_r.at[self.inst, 8], sib).wait_recv()
            else:
                for yy in range(4):
                    for zz in range(2):
                        self.wait(self.slot(yy, zz, 1 - c), 8 + 2 * yy + zz)

        def drain(self):
            ref = self.many(0, 15)
            remote(ref, ref, ag_s.at[self.inst], ag_r.at[self.inst, 0], sib).wait_send()

    def half(h):
        return slice(h * HW, (h + 1) * HW)

    ax = [
        Gather(
            r, (lambda s, r=r: xo.at[r, s]), (lambda s, n, r=r: xo.at[r, pl.ds(s, n)]), by_core
        )
        for r in range(CH)
    ]
    at = Gather(2, (lambda s: tbuf.at[s]), (lambda s, n: tbuf.at[pl.ds(s, n)]), tk)
    ar = [
        [
            Gather(
                3 + HALVES * r + h,
                (lambda s, r=r, h=h: rbuf.at[r, s, :, half(h)]),
                (lambda s, n, r=r, h=h: rbuf.at[r, pl.ds(s, n), :, half(h)]),
                by_core,
            )
            for h in range(HALVES)
        ]
        for r in range(CH)
    ]

    def encode(r):
        rows = xo[r].reshape(CR, D)
        value = jnp.dot(rows, we[...], preferred_element_type=F32) + eb_ref[...]
        pre[r] = value
        acts[r, :, pl.ds(pl.multiple_of(m * FS, FS), FS)] = jnp.maximum(value, 0.0).astype(BF16)

    def act_at(r, l):
        return acts.at[r, :, pl.ds(pl.multiple_of(l * FS, FS), FS)]

    def b_copy(r, k, src, dst, slot, dev):
        return remote(src, dst, b_s.at[r, k], b_r.at[r, slot], dev)

    def b_wait(r, l):
        b_copy(r, 0, act_at(r, l), act_at(r, l), l, sib).wait_recv()

    def b_own(r):
        return [
            (None, b_copy(r, 0, act_at(r, m), pact.at[r], 8, zpl)),
            (x < 3, b_copy(r, 1, act_at(r, m), act_at(r, m), m, xup)),
            (x == 0, b_copy(r, 2, act_at(r, m), act_at(r, m), m, xdn)),
            (m == 3, b_copy(r, 3, act_at(r, m), bact.at[r], 9, xdn)),
        ]

    def b_partner(r):
        return [
            (x < 3, b_copy(r, 4, pact.at[r], act_at(r, mp), mp, xup)),
            (x == 0, b_copy(r, 5, pact.at[r], act_at(r, mp), mp, xdn)),
            (m == 2, b_copy(r, 6, pact.at[r], bact.at[r], 9, xdn)),
        ]

    def b_relay_a(r):
        return [
            (m == 1, 9, b_copy(r, 7, bact.at[r], act_at(r, 3), 3, xdn)),
            (m == 4, 2, b_copy(r, 7, act_at(r, 2), act_at(r, 2), 2, xup)),
            (x == 3, zl, b_copy(r, 7, act_at(r, zl), act_at(r, zl), zl, xdn)),
        ]

    def b_relay_b(r):
        o = 1 - zl
        return [
            (m == 0, 9, b_copy(r, 7, bact.at[r], act_at(r, 3), 3, xdn)),
            (m == 5, 2, b_copy(r, 7, act_at(r, 2), act_at(r, 2), 2, xup)),
            (x == 3, o, b_copy(r, 8, act_at(r, o), act_at(r, o), o, xdn)),
        ]

    def when(cond, fn):
        if cond is None:
            fn()
        else:
            pl.when(cond)(fn)

    def b_start(r):
        for cond, cp in b_own(r):
            when(cond, cp.start)

    def b_step1(r):
        remote(pact.at[r], pact.at[r], b_s.at[r, 0], b_r.at[r, 8], sib).wait_recv()
        for cond, cp in b_partner(r):
            when(cond, cp.start)

        @pl.when(zl == 1)
        def _():
            acts[r, :, pl.ds(pl.multiple_of(mp * FS, FS), FS)] = pact[r]

    def b_pass(r, relays):
        for cond, slot, cp in relays(r):

            def go(slot=slot, cp=cp):
                if isinstance(slot, int) and slot == 9:
                    remote(bact.at[r], bact.at[r], b_s.at[r, 0], b_r.at[r, 9], sib).wait_recv()
                else:
                    b_wait(r, slot)
                cp.start()

            when(cond, go)

    def b_finish(r):
        for cond, slots in ((x == 1, (0, 1)), (x == 2, (0, 1, 3)), (x == 3, (2, 3, 4, 5))):
            when(cond, lambda slots=slots: [b_wait(r, l) for l in slots] and None)

    def b_drain(r):
        for cond, cp in b_own(r) + b_partner(r):
            when(cond, cp.wait_send)
        for cond, _, cp in b_relay_a(r) + b_relay_b(r):
            when(cond, cp.wait_send)

    def clear():
        for l in range(1, LAYERS):

            @pl.when(l > m)
            def _(l=l):
                acts[:, :, l * FS : (l + 1) * FS] = jnp.zeros((CH, CR, FS), BF16)

    def norm_copy(k):
        return remote(nrecv.at[m], nrecv.at[m], n_s.at[k], n_r.at[m], ((m + k) % LAYERS, t))

    def norms(lo, hi):
        for k in range(lo, hi):
            local[4 + k].wait()

        @pl.loop(lo, hi)
        def _(l):
            part = jnp.zeros((FS, 128), F32)
            for j in range(D // 128):
                v = w[pl.ds(pl.multiple_of(l * FS, FS), FS), j * 128 : (j + 1) * 128].astype(F32)
                part = part + v * v
            row = lax.dot_general(
                jnp.ones((8, 128), F32), part, NT_DIMS,
                preferred_element_type=F32, precision=lax.Precision.HIGHEST,
            )
            keep = jnp.where(l <= m, 1.0, 0.0).astype(F32)
            nrecv[m, pl.ds(l, 1), :] = row[0:1] * keep

        if hi == LAYERS:
            for k in range(1, LAYERS):
                norm_copy(k).start()

    def norms_finish():
        for k in range(1, LAYERS):
            s = (m + k) % LAYERS
            remote(nrecv.at[s], nrecv.at[s], n_s.at[0], n_r.at[s], sib).wait_recv()
        total = nrecv[0]
        for s in range(1, LAYERS):
            total = total + nrecv[s]
        no_ref[...] = jnp.sqrt(total + 1e-06)

    def decode(r, h):
        rows = jnp.concatenate(
            [
                acts[r, pl.ds(pl.multiple_of((1 - c) * 128, 128), 128), :],
                acts[r, pl.ds(pl.multiple_of(c * 128, 128), 128), :],
            ],
            axis=0,
        )

        @pl.loop(h * HS, (h + 1) * HS)
        def _(n):
            part = jnp.dot(
                rows, w[:, pl.ds(pl.multiple_of(n * NT, NT), NT)], preferred_element_type=F32
            )
            sibs[r, n] = part[:128].astype(BF16)
            opart[r, n] = part[128:]
            remote(sibs.at[r, n], sibr.at[r, n], cs_s.at[r, n], cs_r.at[r, n], sib).start()

    def cols(n):
        return slice(n * NT, (n + 1) * NT)

    def steps(h):
        return range(h * HS, (h + 1) * HS)

    def chip_sum(r, q, n):
        rows = pl.ds(pl.multiple_of(q * PR, PR), PR)
        return opart[r, n, rows, :] + sibr[r, n, rows, :].astype(F32)

    def y_copy(r, h, k):
        dev = yup if k in (0, 2, 3) else ydn
        src, dst = ys.at[r, k, :, half(h)], yr.at[r, k, :, half(h)]
        return remote(src, dst, cy_s.at[r, h], cy_r.at[r, h, k], dev)

    def y_wait(r, h, k):
        y_copy(r, h, k).wait_recv()

    def c_a(r, h):
        for n in steps(h):
            remote(sibr.at[r, n], sibr.at[r, n], cs_s.at[r, n], cs_r.at[r, n], sib).wait_recv()
        for k, q in ((0, 2 * yo), (1, 2 * yo + 1), (3, 2 * yp + 1), (4, 2 * ym)):
            for n in steps(h):
                ys[r, k, :, cols(n)] = chip_sum(r, q, n).astype(BF16)
            y_copy(r, h, k).start()

    def c_b(r, h):
        for k, q, i in ((2, 2 * yp, 0), (5, 2 * ym + 1, 1)):
            y_wait(r, h, i)
            for n in steps(h):
                ys[r, k, :, cols(n)] = (
                    chip_sum(r, q, n) + yr[r, i, :, cols(n)].astype(F32)
                ).astype(BF16)
            y_copy(r, h, k).start()

    def z_copy(r, h):
        src, dst = zs.at[r, :, half(h)], zr.at[r, :, half(h)]
        return remote(src, dst, cz_s.at[r, h], cz_r.at[r, h], zpt)

    def c_c(r, h):
        for k in (2, 3, 4, 5):
            y_wait(r, h, k)
        for n in steps(h):
            other = chip_sum(r, 2 * y + 1 - zh, n)
            other = other + yr[r, 3 - zh, :, cols(n)].astype(F32)
            other = other + yr[r, 5 - zh, :, cols(n)].astype(F32)
            zs[r, :, cols(n)] = other.astype(BF16)
        z_copy(r, h).start()
        for n in steps(h):
            mine = chip_sum(r, 2 * y + zh, n)
            mine = mine + yr[r, 2 + zh, :, cols(n)].astype(F32)
            mine = mine + yr[r, 4 + zh, :, cols(n)].astype(F32)
            dkeep[r, :, cols(n)] = mine

    def pick_targets():
        for r in range(CH):
            ids = lax.broadcasted_iota(jnp.int32, (PR, ROWS), 0) + (2 * PR * t + PR * r)
            pick = (jnp.broadcast_to(order_ref[...], (PR, ROWS)) == ids).astype(F32).astype(BF16)
            wanted = jnp.dot(pick, tbuf[...].reshape(ROWS, D), preferred_element_type=F32)
            tpick[r] = db_ref[...] - wanted

    def c_d(r, h):
        z_copy(r, h).wait_recv()
        resid = (dkeep[r, :, half(h)] + zr[r, :, half(h)].astype(F32) + tpick[r, :, half(h)]) * SCALE
        rbuf[r, own_core, :, half(h)] = resid.astype(BF16)
        ar[r][h].start()

    def f_copy(r, k, src, slot, dev):
        return remote(src, frecv.at[r, slot], f_s.at[r, k], f_r.at[r, slot], dev)

    def f_wait(r, slot):
        remote(frecv.at[r, slot], frecv.at[r, slot], f_s.at[r, 0], f_r.at[r, slot], sib).wait_recv()

    def f_sends(r, name):
        return {
            "a1": lambda: [f_copy(r, 0, gb.at[r, 0], 0, xdn)],
            "s1": lambda: [f_copy(r, 1, gb.at[r, 1], 1, xdn)],
            "a2": lambda: [
                f_copy(r, 0, gb.at[r, 0], 2, xup),
                f_copy(r, 1, gb.at[r, 1], 4, xdn),
            ],
            "a3": lambda: [f_copy(r, 3, gb.at[r, 3], 4, xup), f_copy(r, 2, gb.at[r, 2], 4, xdn)],
            "b2": lambda: [f_copy(r, 3, gb.at[r, 3], 1, xdn)],
            "s2": lambda: [f_copy(r, 2, gb.at[r, 2], 0, xdn)],
            "b3": lambda: [f_copy(r, 4 + l, gb.at[r, 4 + l], l, xdn) for l in (0, 1)],
            "c3": lambda: [f_copy(r, 1, gb.at[r, 1], 3, xup)],
            "s3": lambda: [f_copy(r, 0, gb.at[r, 0], 2, xup)],
            "r0": lambda: [f_copy(r, 7, frecv.at[r, 4], 2, xup)],
        }[name]()

    def f_go(r, name, before=None):
        @pl.when(x == int(name[1]))
        def _():
            if before is not None:
                before()
            for cp in f_sends(r, name):
                cp.start()

    def grads(r, i):
        @pl.when(i <= x)
        def _():
            p = (i + x // 3) % 3 if i < 3 else 3
            g = lax.dot_general(
                rbuf[r].reshape(CR, D), w[pl.ds(pl.multiple_of(p * 2 * FS, 2 * FS), 2 * FS), :],
                NT_DIMS, preferred_element_type=F32,
            )

            @pl.when(x != i)
            def _():
                gb[r, 2 * p] = g[:, :FS].astype(BF16)
                gb[r, 2 * p + 1] = g[:, FS:].astype(BF16)

            @pl.when(x == i)
            def _():
                gown[r, 0] = g[:, :FS]
                gown[r, 1] = g[:, FS:] * zl.astype(F32)

        def add(pairs):
            def fn():
                for l, slot in pairs:
                    f_wait(r, slot)
                    gb[r, l] = (gb[r, l].astype(F32) + frecv[r, slot].astype(F32)).astype(BF16)

            return fn

        if i == 0:
            for name in ("a1", "a2", "a3"):
                f_go(r, name)
        if i == 1:
            f_go(r, "b2")
            f_go(r, "b3")
        if i == 2:
            f_go(r, "c3")

    def f_add(r):
        def add(l, slot):
            def fn():
                f_wait(r, slot)
                gb[r, l] = (gb[r, l].astype(F32) + frecv[r, slot].astype(F32)).astype(BF16)

            return fn

        f_go(r, "s1", add(1, 4))
        f_go(r, "s2", add(2, 4))
        f_go(r, "s3", add(0, 2))

    def f_relay(r):
        f_go(r, "r0", lambda: f_wait(r, 4))

    def f_zcopy(r):
        return remote(fzs.at[r], fzr.at[r], fz_s.at[r], fz_r.at[r], zpl)

    def f_fin1(r):
        for cond, adds in (
            (x == 0, ((0, 0), (1, 1), (0, 2), (1, 3))),
            (x == 1, ((0, 0), (1, 1), (1, 2))),
            (x == 2, ((0, 0), (1, 1))),
        ):

            @pl.when(cond)
            def _(adds=adds):
                for j, slot in adds:
                    f_wait(r, slot)
                    gown[r, j] = gown[r, j] + frecv[r, slot].astype(F32)

        fzs[r] = gown[r, 1 - zl].astype(BF16)
        f_zcopy(r).start()

    def f_fin2(r):
        remote(fzr.at[r], fzr.at[r], fz_s.at[r], fz_r.at[r], sib).wait_recv()
        total = gown[r, zl] + fzr[r].astype(F32)
        norm = no_ref[pl.ds(m, 1), :]
        grad = jnp.where(pre[r] > 0, total + norm * SCALE, 0.0)
        go[r] = grad.astype(BF16)
        fsum = jnp.sum(grad, axis=0, keepdims=True)
        fo[...] = fsum if r == 0 else fo[...] + fsum

    def flip(r):
        @pl.loop(0, LAYERS)
        def _(l):
            block = acts[r, :, pl.ds(pl.multiple_of(l * FS, FS), FS)]
            act_t[l, :, r * CR : (r + 1) * CR] = block.T

    def dec_zero():
        for l in range(1, LAYERS):

            @pl.when(l > m)
            def _(l=l):
                do[l] = jnp.zeros((FS, D), BF16)

    def dec_grads(lo, hi):
        @pl.loop(lo, hi)
        def _(l):
            @pl.when(l <= m)
            def _():
                a_t = act_t[l]
                sums = jnp.dot(a_t, jnp.ones((ROWS, 128), BF16), preferred_element_type=F32)
                pick = (lax.broadcasted_iota(jnp.int32, (LAYERS, 128), 0) == l).astype(F32)
                norm = lax.dot_general(
                    no_ref[...], pick, TN_DIMS,
                    preferred_element_type=F32, precision=lax.Precision.HIGHEST,
                )
                factor = jnp.concatenate([sums * SCALE / norm] * 4, axis=1)
                rows = pl.ds(pl.multiple_of(l * FS, FS), FS)
                for n in range(NSTEPS):
                    part = jnp.dot(
                        a_t, rbuf[:, :, :, cols(n)].reshape(ROWS, NT), preferred_element_type=F32
                    )
                    do[l, :, cols(n)] = (part + factor * w[rows, cols(n)].astype(F32)).astype(BF16)

    def out_sum():
        ones = jnp.ones((8, ROWS), BF16)
        oo[...] = jnp.dot(ones, rbuf[...].reshape(ROWS, D), preferred_element_type=F32)[0:1]

    for k in range(2):
        local[k].wait()
    ax[0].start()
    clear()
    dec_zero()
    ax[0].relay_z()
    ax[0].relay_y()
    ax[1].start()
    norms(0, 4)
    ax[0].relay_zy()
    ax[0].far_y()
    ax[1].relay_z()
    ax[1].relay_y()
    local[2].wait()
    local[3].wait()
    ax[0].finish()
    encode(0)
    b_start(0)
    ax[1].relay_zy()
    ax[1].far_y()
    ax[1].finish()
    encode(1)
    b_step1(0)
    b_start(1)
    at.start()
    b_pass(0, b_relay_a)
    norms(4, 8)
    b_pass(0, b_relay_b)
    at.relay_z()
    at.relay_y()
    b_step1(1)
    b_pass(1, b_relay_a)
    b_finish(0)
    decode(0, 0)
    b_pass(1, b_relay_b)
    at.relay_zy()
    at.far_y()
    c_a(0, 0)
    decode(0, 1)
    c_a(0, 1)
    c_b(0, 0)
    at.finish()
    pick_targets()
    b_finish(1)
    c_b(0, 1)
    c_c(0, 0)
    decode(1, 0)
    c_a(1, 0)
    c_c(0, 1)
    decode(1, 1)
    c_a(1, 1)
    c_d(0, 0)
    c_b(1, 0)
    c_d(0, 1)
    c_b(1, 1)
    ar[0][0].relay_z()
    ar[0][0].relay_y()
    c_c(1, 0)
    ar[0][1].relay_z()
    ar[0][1].relay_y()
    c_c(1, 1)
    ar[0][0].relay_zy()
    ar[0][0].far_y()
    c_d(1, 0)
    ar[0][1].relay_zy()
    ar[0][1].far_y()
    c_d(1, 1)
    flip(0)
    ar[0][0].finish()
    ar[0][1].finish()
    ar[1][0].relay_z()
    ar[1][0].relay_y()
    grads(0, 0)
    ar[1][1].relay_z()
    ar[1][1].relay_y()
    grads(0, 1)
    ar[1][0].relay_zy()
    ar[1][0].far_y()
    grads(0, 2)
    ar[1][1].relay_zy()
    ar[1][1].far_y()
    grads(0, 3)
    flip(1)
    norms_finish()
    ar[1][0].finish()
    ar[1][1].finish()
    f_add(0)
    grads(1, 0)
    grads(1, 1)
    grads(1, 2)
    f_relay(0)
    grads(1, 3)
    out_sum()
    dec_grads(0, 4)
    f_add(1)
    f_relay(1)
    f_fin1(0)
    dec_grads(4, 8)
    f_fin2(0)
    f_fin1(1)
    f_fin2(1)

    for g in ax + [at] + ar[0] + ar[1]:
        g.drain()
    for r in range(CH):
        b_drain(r)
        for n in range(NSTEPS):
            remote(sibs.at[r, n], sibr.at[r, n], cs_s.at[r, n], cs_r.at[r, n], sib).wait_send()
        for h in range(HALVES):
            ref = ys.at[r, :, :, half(h)]
            remote(ref, ref, cy_s.at[r, h], cy_r.at[r, h, 0], sib).wait_send()
            z_copy(r, h).wait_send()
        for name in ("a1", "s1", "a2", "a3", "b2", "s2", "b3", "c3", "s3", "r0"):

            @pl.when(x == int(name[1]))
            def _(name=name):
                for cp in f_sends(r, name):
                    cp.wait_send()

        f_zcopy(r).wait_send()
    for k in range(1, LAYERS):
        norm_copy(k).wait_send()


def run_main(x, tgt, order, we, eb, w, db):
    any_spec = pl.BlockSpec(memory_space=pl.ANY)
    vmem = pl.BlockSpec(memory_space=pltpu.VMEM)
    dma = pltpu.SemaphoreType.DMA
    return pl.pallas_call(
        main_kernel,
        out_shape=(
            pltpu.VMEM((CH, TOKS, PR, D), BF16),
            pltpu.VMEM((CH, CR, FS), BF16),
            pltpu.VMEM((LAYERS, FS, D), BF16),
            pltpu.VMEM((1, FS), F32),
            pltpu.VMEM((1, D), F32),
        ),
        in_specs=[any_spec, any_spec, vmem, any_spec, vmem, any_spec, vmem],
        out_specs=(vmem,) * 5,
        scratch_shapes=[
            pltpu.VMEM((TOKS, 2 * PR, D), BF16),
            pltpu.VMEM((CH, TOKS, PR, D), BF16),
            pltpu.VMEM((CH, CR, D), BF16),
            pltpu.VMEM((CH, CR, FS), BF16),
            pltpu.VMEM((CH, CR, FS), BF16),
            pltpu.VMEM((CH, CR, FS), F32),
            pltpu.VMEM((D, FS), BF16),
            pltpu.VMEM((LAYERS * FS, D), BF16),
            pltpu.VMEM((CH, NSTEPS, 128, NT), F32),
            pltpu.VMEM((CH, NSTEPS, 128, NT), BF16),
            pltpu.VMEM((CH, NSTEPS, 128, NT), BF16),
            pltpu.VMEM((CH, 6, PR, D), BF16),
            pltpu.VMEM((CH, 6, PR, D), BF16),
            pltpu.VMEM((CH, PR, D), BF16),
            pltpu.VMEM((CH, PR, D), BF16),
            pltpu.VMEM((CH, PR, D), F32),
            pltpu.VMEM((CH, PR, D), F32),
            pltpu.VMEM((CH, LAYERS, CR, FS), BF16),
            pltpu.VMEM((CH, 2, CR, FS), F32),
            pltpu.VMEM((CH, 5, CR, FS), BF16),
            pltpu.VMEM((CH, CR, FS), BF16),
            pltpu.VMEM((CH, CR, FS), BF16),
            pltpu.VMEM((LAYERS, LAYERS, FS), F32),
            pltpu.VMEM((LAYERS, FS), F32),
            pltpu.VMEM((LAYERS, FS, ROWS), BF16),
            dma((4 + LAYERS,)), dma((3 + CH * HALVES,)), dma((3 + CH * HALVES, TOKS)),
            dma((CH, 9)), dma((CH, 10)), dma((CH, NSTEPS)), dma((CH, NSTEPS)),
            dma((CH, HALVES)), dma((CH, HALVES, 6)), dma((CH, HALVES)), dma((CH, HALVES)),
            dma((CH, 8)), dma((CH, 5)), dma((CH,)), dma((CH,)),
            dma((LAYERS,)), dma((LAYERS,)),
        ],
        compiler_params=pltpu.CompilerParams(
            collective_id=0, has_side_effects=True, vmem_limit_bytes=46 << 20
        ),
        name="window",
    )(x, tgt, order, we, eb, w, db)


def tail_kernel(x_ref, g_ref, d_ref, f_ref, o_ref, dw_hbm, dwe_hbm, fg_hbm, og_hbm, enc, sems):
    copies = [
        pltpu.make_async_copy(d_ref, dw_hbm.at[0], sems.at[0]),
        pltpu.make_async_copy(f_ref, fg_hbm, sems.at[2]),
        pltpu.make_async_copy(o_ref, og_hbm, sems.at[3]),
    ]
    for cp in copies:
        cp.start()
    g = g_ref[...].reshape(ROWS, FS).T
    for n in range(NSTEPS):
        cs = slice(n * NT, (n + 1) * NT)
        part = jnp.dot(g, x_ref[:, :, :, cs].reshape(ROWS, NT), preferred_element_type=F32)
        enc[cs, :] = part.astype(BF16).T
    copies.append(pltpu.make_async_copy(enc, dwe_hbm.at[0], sems.at[1]))
    copies[-1].start()
    for cp in copies:
        cp.wait()


def run_tail(xs, gl, dec, fg, og):
    any_spec = pl.BlockSpec(memory_space=pl.ANY)
    vmem = pl.BlockSpec(memory_space=pltpu.VMEM)
    return pl.pallas_call(
        tail_kernel,
        out_shape=(
            jax.ShapeDtypeStruct((1, LAYERS, FS, D), BF16),
            jax.ShapeDtypeStruct((1, D, FS), BF16),
            jax.ShapeDtypeStruct((1, FS), F32),
            jax.ShapeDtypeStruct((1, D), F32),
        ),
        in_specs=[vmem] * 5,
        out_specs=(any_spec,) * 4,
        scratch_shapes=[pltpu.VMEM((D, FS), BF16), pltpu.SemaphoreType.DMA((4,))],
        compiler_params=pltpu.CompilerParams(vmem_limit_bytes=20 << 20),
        name="weights",
    )(xs, gl, dec, fg, og)


def on_device(x, tgt, order, we, eb, w, db):
    xs, gl, dec, fg, og = run_main(x, tgt, order[None], we, eb, w, db)
    dw, dwe, fg, og = run_tail(xs, gl, dec, fg, og)
    return dwe, fg, dw, og


def solution(mesh):
    placed = (
        P("layer", "tok", None),
        P("layer", "tok", None),
        P(),
        P("layer", None, "tok"),
        P("layer", "tok"),
        P("layer", None, "tok", None),
        P("layer", None),
    )
    return jax.shard_map(
        on_device,
        mesh=mesh,
        in_specs=placed,
        out_specs=(
            P("layer", None, "tok"),
            P("layer", "tok"),
            P("layer", None, "tok", None),
            P("layer", None),
        ),
        check_vma=False,
    )
```

time: 120 us -> 102 us (0.85)
  Pallas kernels: 115 us -> 101 us
  local copies, waits for them, and re-layouts: 3.23 us -> 0 us
    pallas_call x2, Pallas kernels: 115 us -> 101 us  [the longest x1 97 us: run_main(): pl.pallas_call(main_kernel, out_shape=(pltpu.VMEM((CH, TOKS, PR, D), BF16...]
    unnamed x6 -> x0, local copies, waits for them, and re-layouts: 3.23 us -> none
where the time goes in v2:
time: 102 us
  Pallas kernels  101 us (99%)
    pallas_call x1, Pallas kernels, run_main(): pl.pallas_call(main_kernel, out_shape=(pltpu.VMEM((CH, TOKS, PR, D), BF16...  97 us
    pallas_call x1, Pallas kernels, run_tail(): pl.pallas_call(tail_kernel, out_shape=(jax.ShapeDtypeStruct((1, LAYERS, F...  3.78 us

profile of v2, /device:TPU:1, one launch (start us, length us, event | category | flops | bytes accessed | tf_op | source)
XLA Modules:
  0.0 101.5 jit_solution(1732005930817871845)
XLA Ops:
  0.6 97.0 %window.1 = (bf16[2,16,16,2048]{3,2,1,0:T(8,128)(2,1)S(1)}, bf16[2,256,256]{2,1,0:T(8,128)(2,1)S(1)}, bf16[8,256,2048]{2,1,0:T(8,128)(2,1)S(1)}, f32[1,256]{1,0:T(1,128)S(1)}, f32[1,2048]{1,0:T(1,128)S(1)}) custom-call(bf16[1,32,2048]{2,1,0:T(8,128)(2,1)} %x_hbm.1, bf16[1,32,2048]{2,1,0:T(8,128)(2,1)} %t_hbm.1, s32[1,512]{1,0:T(1,128)} %bitcast.1, ...), custom_call_target="tpu_custom_call" | custom-call | tf_op jit(solution)/shard_map/window/pallas_call | solution.py:657
  97.6 3.8 %weights.1 = (bf16[1,8,256,2048]{3,2,1,0:T(8,128)(2,1)}, bf16[1,2048,256]{2,1,0:T(8,128)(2,1)}, f32[1,256]{1,0:T(1,128)}, f32[1,2048]{1,0:T(1,128)}) custom-call(bf16[2,16,16,2048]{3,2,1,0:T(8,128)(2,1)S(1)} %get-tuple-element.13.x_ref, bf16[2,256,256]{2,1,0:T(8,128)(2,1)S(1)} %get-tuple-element.14.g_ref, bf16[8,256,2048]{2,1,0:T(8,128)(2,1)S(1)} %get-tuple-element.15.d_ref, ...), custom_call_target="tpu_custom_call" | custom-call | tf_op jit(solution)/shard_map/weights/pallas_call | solution.py:729

commit v3 on v2

--- a/solution.py
+++ b/solution.py
@@ -32,25 +32,25 @@
     x_hbm, t_hbm, order_ref, we_hbm, eb_ref, w_hbm, db_ref,
     xo, go, do, fo, oo,
     tbuf, rbuf, acts, pact, bact, pre, we, w,
-    opart, sibs, sibr, ys, yr, zs, zr, dkeep, tpick,
+    opart, sibs, sibr, ys, yr, hit,
     gb, gown, frecv, fzs, fzr, nrecv, no_ref, act_t,
-    lsem, ag_s, ag_r, b_s, b_r, cs_s, cs_r, cy_s, cy_r, cz_s, cz_r,
+    lsem, ag_s, ag_r, b_s, b_r, cs_s, cs_r, cy_s, cy_r,
     f_s, f_r, fz_s, fz_r, n_s, n_r,
 ):
     m, t = lax.axis_index("layer"), lax.axis_index("tok")
     x, zl = m // 2, m % 2
     y, zh, c = t // 4, (t // 2) % 2, t % 2
-    yp, ym, yo = (y + 1) % 4, (y + 3) % 4, (y + 2) % 4
     xp, xm = (x + 1) % 4, (x + 3) % 4
 
     def tk(yy, zz, cc):
         return 4 * yy + 2 * zz + cc
 
-    def by_core(yy, zz, cc):
-        return 8 * cc + 2 * yy + zz
-
-    sib, zpt = (m, tk(y, zh, 1 - c)), (m, tk(y, 1 - zh, c))
-    yup, ydn = (m, tk(yp, zh, c)), (m, tk(ym, zh, c))
+    sib = (m, tk(y, zh, 1 - c))
+    others = [
+        ((y + dy) % 4, (zh + dz) % 2) for dy, dz in ((2, 1), (1, 1), (3, 1), (2, 0), (0, 1), (1, 0), (3, 0))
+    ]
+    peers = [(2 * yy + zz, (m, tk(yy, zz, c))) for yy, zz in others]
+    place = 2 * y + zh
     xup, xdn = (2 * xp + zl, t), (2 * xm + zl, t)
     mp = m + 1 - 2 * zl
     zpl = (mp, t)
@@ -67,101 +67,55 @@
         cp.start()
         local.append(cp)
 
-    own_core = by_core(y, zh, c)
+    own_core = 8 * c + place
     for r in range(CH):
         fetch(x_hbm.at[0, pl.ds(r * PR, PR)], xo.at[r, own_core], r)
     fetch(we_hbm.at[0], we, 2)
-    fetch(t_hbm.at[0], tbuf.at[t], 3)
+    fetch(t_hbm.at[0], tbuf.at[pl.ds(0, 2 * PR)], 3)
     for l in range(LAYERS):
         fetch(w_hbm.at[0, l], w.at[pl.ds(l * FS, FS)], 4 + l)
 
     barrier = pltpu.get_barrier_semaphore()
-    for dev in (sib, zpt, yup, ydn):
+    for dev in [sib] + [dev for _, dev in peers]:
         pl.semaphore_signal(barrier, inc=1, device_id=dev, device_id_type=MESH)
     for k in range(1, LAYERS):
         pl.semaphore_signal(barrier, inc=1, device_id=((m + k) % LAYERS, t), device_id_type=MESH)
-    pl.semaphore_wait(barrier, 4 + LAYERS - 1)
+    pl.semaphore_wait(barrier, 8 + LAYERS - 1)
 
     class Gather:
-        def __init__(self, inst, at, many, slot):
-            self.inst, self.at, self.many, self.slot = inst, at, many, slot
-
-        def send(self, slot, dev, sem):
-            remote(self.at(slot), self.at(slot), ag_s.at[self.inst], ag_r.at[self.inst, sem], dev).start()
-
-        def wait(self, slot, sem):
-            remote(self.at(slot), self.at(slot), ag_s.at[self.inst], ag_r.at[self.inst, sem], sib).wait_recv()
-
-        def to_sib(self, yy, zz):
-            shared = self.slot is by_core
-            self.send(self.slot(yy, zz, c), sib, 8 if shared else 8 + 2 * yy + zz)
-
-        def to(self, yy, zz, *devs):
-            for dev in devs:
-                self.send(self.slot(yy, zz, c), dev, 2 * yy + zz)
-
-        def take(self, yy, zz):
-            self.wait(self.slot(yy, zz, c), 2 * yy + zz)
+        def __init__(self, inst, at):
+            self.inst, self.at = inst, at
+
+        def copy(self, core, first, number, k, dev):
+            ref = self.at(core, first, number)
+            return remote(ref, ref, ag_s.at[self.inst, k], ag_r.at[self.inst, k], dev)
 
         def start(self):
-            self.to(y, zh, zpt, yup, ydn)
-            self.to_sib(y, zh)
-
-        def relay_z(self):
-            self.take(y, 1 - zh)
-            self.to(y, 1 - zh, yup, ydn)
-            self.to_sib(y, 1 - zh)
-
-        def relay_y(self):
-            self.take(ym, zh)
-            self.to(ym, zh, yup)
-            self.to_sib(ym, zh)
-            self.take(yp, zh)
-            self.to_sib(yp, zh)
-
-        def relay_zy(self):
-            self.take(yp, 1 - zh)
-            self.to(yp, 1 - zh, ydn)
-            self.to_sib(yp, 1 - zh)
-            self.take(ym, 1 - zh)
-            self.to_sib(ym, 1 - zh)
-
-        def far_y(self):
-            self.take(yo, zh)
-            self.to_sib(yo, zh)
+            for _, dev in peers:
+                self.copy(c, place, 1, 0, dev).start()
+
+        def sent(self):
+            self.copy(c, 0, 7, 0, sib).wait_send()
+
+        def take(self):
+            self.copy(c, 0, 7, 0, sib).wait_recv()
+            self.copy(c, 0, 8, 1, sib).start()
 
         def finish(self):
-            self.take(yo, 1 - zh)
-            self.to_sib(yo, 1 - zh)
-            if self.slot is by_core:
-                ref = self.many(8 * (1 - c), 8)
-                remote(ref, ref, ag_s.at[self.inst], ag_r.at[self.inst, 8], sib).wait_recv()
-            else:
-                for yy in range(4):
-                    for zz in range(2):
-                        self.wait(self.slot(yy, zz, 1 - c), 8 + 2 * yy + zz)
+            self.copy(1 - c, 0, 8, 1, sib).wait_recv()
 
         def drain(self):
-            ref = self.many(0, 15)
-            remote(ref, ref, ag_s.at[self.inst], ag_r.at[self.inst, 0], sib).wait_send()
+            self.copy(c, 0, 8, 1, sib).wait_send()
 
     def half(h):
         return slice(h * HW, (h + 1) * HW)
 
-    ax = [
-        Gather(
-            r, (lambda s, r=r: xo.at[r, s]), (lambda s, n, r=r: xo.at[r, pl.ds(s, n)]), by_core
-        )
-        for r in range(CH)
-    ]
-    at = Gather(2, (lambda s: tbuf.at[s]), (lambda s, n: tbuf.at[pl.ds(s, n)]), tk)
+    ax = [Gather(r, lambda cc, f, n, r=r: xo.at[r, pl.ds(8 * cc + f, n)]) for r in range(CH)]
     ar = [
         [
             Gather(
-                3 + HALVES * r + h,
-                (lambda s, r=r, h=h: rbuf.at[r, s, :, half(h)]),
-                (lambda s, n, r=r, h=h: rbuf.at[r, pl.ds(s, n), :, half(h)]),
-                by_core,
+                CH + HALVES * r + h,
+                lambda cc, f, n, r=r, h=h: rbuf.at[r, pl.ds(8 * cc + f, n), :, half(h)],
             )
             for h in range(HALVES)
         ]
@@ -262,7 +216,11 @@
                 acts[:, :, l * FS : (l + 1) * FS] = jnp.zeros((CH, CR, FS), BF16)
 
     def norm_copy(k):
-        return remote(nrecv.at[m], nrecv.at[m], n_s.at[k], n_r.at[m], ((m + k) % LAYERS, t))
+        return remote(nrecv.at[m], nrecv.at[m], n_s.at[0], n_r.at[0], ((m + k) % LAYERS, t))
+
+    def norm_all():
+        ref = nrecv.at[pl.ds(0, LAYERS - 1)]
+        return remote(ref, ref, n_s.at[0], n_r.at[0], sib)
 
     def norms(lo, hi):
         for k in range(lo, hi):
@@ -286,9 +244,7 @@
                 norm_copy(k).start()
 
     def norms_finish():
-        for k in range(1, LAYERS):
-            s = (m + k) % LAYERS
-            remote(nrecv.at[s], nrecv.at[s], n_s.at[0], n_r.at[s], sib).wait_recv()
+        norm_all().wait_recv()
         total = nrecv[0]
         for s in range(1, LAYERS):
             total = total + nrecv[s]
@@ -308,9 +264,12 @@
             part = jnp.dot(
                 rows, w[:, pl.ds(pl.multiple_of(n * NT, NT), NT)], preferred_element_type=F32
             )
+            part = part - jnp.dot(
+                hit[r], tbuf[:, pl.ds(pl.multiple_of(n * NT, NT), NT)], preferred_element_type=F32
+            )
             sibs[r, n] = part[:128].astype(BF16)
             opart[r, n] = part[128:]
-            remote(sibs.at[r, n], sibr.at[r, n], cs_s.at[r, n], cs_r.at[r, n], sib).start()
+            remote(sibs.at[r, n], sibr.at[r, n], cs_s.at[r], cs_r.at[r, h], sib).start()
 
     def cols(n):
         return slice(n * NT, (n + 1) * NT)
@@ -322,61 +281,46 @@
         rows = pl.ds(pl.multiple_of(q * PR, PR), PR)
         return opart[r, n, rows, :] + sibr[r, n, rows, :].astype(F32)
 
-    def y_copy(r, h, k):
-        dev = yup if k in (0, 2, 3) else ydn
-        src, dst = ys.at[r, k, :, half(h)], yr.at[r, k, :, half(h)]
-        return remote(src, dst, cy_s.at[r, h], cy_r.at[r, h, k], dev)
-
-    def y_wait(r, h, k):
-        y_copy(r, h, k).wait_recv()
+    def c_copy(r, h, src, dst, dev):
+        return remote(
+            ys.at[r, src, :, half(h)], yr.at[r, dst, :, half(h)], cy_s.at[r, h], cy_r.at[r, h], dev
+        )
+
+    def c_all(r, h):
+        ref = ys.at[r, pl.ds(0, 7), :, half(h)]
+        return remote(ref, ref, cy_s.at[r, h], cy_r.at[r, h], sib)
 
     def c_a(r, h):
+        ref = sibr.at[r, pl.ds(h * HS, HS)]
+        remote(ref, ref, cs_s.at[r], cs_r.at[r, h], sib).wait_recv()
+        for q, dev in peers:
+            for n in steps(h):
+                ys[r, q, :, cols(n)] = chip_sum(r, q, n).astype(BF16)
+            c_copy(r, h, q, place, dev).start()
+
+    def place_targets():
+        tbuf[2 * PR :, :] = jnp.zeros((128 - 2 * PR, D), BF16)
+        own_rows = (
+            lax.broadcasted_iota(jnp.int32, (ROWS, 128), 0)
+            == lax.broadcasted_iota(jnp.int32, (ROWS, 128), 1) + 2 * PR * t
+        ) & (lax.broadcasted_iota(jnp.int32, (ROWS, 128), 1) < 2 * PR)
+        own_rows = own_rows.astype(F32).astype(BF16)
+        row = lax.broadcasted_iota(jnp.int32, (CR, ROWS), 0)
+        core = (row // 128 + 1 - c) % 2
+        base = 2 * PR * (2 * ((row % 128) // PR) + core) + row % PR
+        wanted = jnp.broadcast_to(order_ref[...], (CR, ROWS))
+        for r in range(CH):
+            found = (wanted == base + PR * r).astype(F32).astype(BF16)
+            hit[r] = jnp.dot(found, own_rows, preferred_element_type=F32).astype(BF16)
+
+    def c_d(r, h):
+        c_all(r, h).wait_recv()
         for n in steps(h):
-            remote(sibr.at[r, n], sibr.at[r, n], cs_s.at[r, n], cs_r.at[r, n], sib).wait_recv()
-        for k, q in ((0, 2 * yo), (1, 2 * yo + 1), (3, 2 * yp + 1), (4, 2 * ym)):
-            for n in steps(h):
-                ys[r, k, :, cols(n)] = chip_sum(r, q, n).astype(BF16)
-            y_copy(r, h, k).start()
-
-    def c_b(r, h):
-        for k, q, i in ((2, 2 * yp, 0), (5, 2 * ym + 1, 1)):
-            y_wait(r, h, i)
-            for n in steps(h):
-                ys[r, k, :, cols(n)] = (
-                    chip_sum(r, q, n) + yr[r, i, :, cols(n)].astype(F32)
-                ).astype(BF16)
-            y_copy(r, h, k).start()
-
-    def z_copy(r, h):
-        src, dst = zs.at[r, :, half(h)], zr.at[r, :, half(h)]
-        return remote(src, dst, cz_s.at[r, h], cz_r.at[r, h], zpt)
-
-    def c_c(r, h):
-        for k in (2, 3, 4, 5):
-            y_wait(r, h, k)
-        for n in steps(h):
-            other = chip_sum(r, 2 * y + 1 - zh, n)
-            other = other + yr[r, 3 - zh, :, cols(n)].astype(F32)
-            other = other + yr[r, 5 - zh, :, cols(n)].astype(F32)
-            zs[r, :, cols(n)] = other.astype(BF16)
-        z_copy(r, h).start()
-        for n in steps(h):
-            mine = chip_sum(r, 2 * y + zh, n)
-            mine = mine + yr[r, 2 + zh, :, cols(n)].astype(F32)
-            mine = mine + yr[r, 4 + zh, :, cols(n)].astype(F32)
-            dkeep[r, :, cols(n)] = mine
-
-    def pick_targets():
-        for r in range(CH):
-            ids = lax.broadcasted_iota(jnp.int32, (PR, ROWS), 0) + (2 * PR * t + PR * r)
-            pick = (jnp.broadcast_to(order_ref[...], (PR, ROWS)) == ids).astype(F32).astype(BF16)
-            wanted = jnp.dot(pick, tbuf[...].reshape(ROWS, D), preferred_element_type=F32)
-            tpick[r] = db_ref[...] - wanted
-
-    def c_d(r, h):
-        z_copy(r, h).wait_recv()
-        resid = (dkeep[r, :, half(h)] + zr[r, :, half(h)].astype(F32) + tpick[r, :, half(h)]) * SCALE
-        rbuf[r, own_core, :, half(h)] = resid.astype(BF16)
+            total = chip_sum(r, place, n)
+            for q, _ in peers:
+                total = total + yr[r, q, :, cols(n)].astype(F32)
+            resid = (total + db_ref[:, cols(n)]) * SCALE
+            rbuf[r, own_core, :, cols(n)] = resid.astype(BF16)
         ar[r][h].start()
 
     def f_copy(r, k, src, slot, dev):
@@ -531,113 +475,82 @@
     ax[0].start()
     clear()
     dec_zero()
-    ax[0].relay_z()
-    ax[0].relay_y()
+    norms(0, 4)
+    place_targets()
+    ax[0].sent()
     ax[1].start()
-    norms(0, 4)
-    ax[0].relay_zy()
-    ax[0].far_y()
-    ax[1].relay_z()
-    ax[1].relay_y()
     local[2].wait()
     local[3].wait()
+    ax[0].take()
     ax[0].finish()
     encode(0)
     b_start(0)
-    ax[1].relay_zy()
-    ax[1].far_y()
+    ax[1].take()
+    b_step1(0)
+    b_pass(0, b_relay_a)
     ax[1].finish()
     encode(1)
-    b_step1(0)
     b_start(1)
-    at.start()
-    b_pass(0, b_relay_a)
     norms(4, 8)
     b_pass(0, b_relay_b)
-    at.relay_z()
-    at.relay_y()
     b_step1(1)
     b_pass(1, b_relay_a)
     b_finish(0)
     decode(0, 0)
-    b_pass(1, b_relay_b)
-    at.relay_zy()
-    at.far_y()
     c_a(0, 0)
     decode(0, 1)
     c_a(0, 1)
-    c_b(0, 0)
-    at.finish()
-    pick_targets()
+    b_pass(1, b_relay_b)
+    c_d(0, 0)
     b_finish(1)
-    c_b(0, 1)
-    c_c(0, 0)
+    c_d(0, 1)
     decode(1, 0)
     c_a(1, 0)
-    c_c(0, 1)
     decode(1, 1)
     c_a(1, 1)
-    c_d(0, 0)
-    c_b(1, 0)
-    c_d(0, 1)
-    c_b(1, 1)
-    ar[0][0].relay_z()
-    ar[0][0].relay_y()
-    c_c(1, 0)
-    ar[0][1].relay_z()
-    ar[0][1].relay_y()
-    c_c(1, 1)
-    ar[0][0].relay_zy()
-    ar[0][0].far_y()
+    ar[0][0].take()
+    ar[0][1].take()
     c_d(1, 0)
-    ar[0][1].relay_zy()
-    ar[0][1].far_y()
     c_d(1, 1)
-    flip(0)
     ar[0][0].finish()
     ar[0][1].finish()
-    ar[1][0].relay_z()
-    ar[1][0].relay_y()
     grads(0, 0)
-    ar[1][1].relay_z()
-    ar[1][1].relay_y()
     grads(0, 1)
-    ar[1][0].relay_zy()
-    ar[1][0].far_y()
     grads(0, 2)
-    ar[1][1].relay_zy()
-    ar[1][1].far_y()
     grads(0, 3)
-    flip(1)
+    ar[1][0].take()
+    ar[1][1].take()
+    f_add(0)
+    flip(0)
     norms_finish()
     ar[1][0].finish()
     ar[1][1].finish()
-    f_add(0)
     grads(1, 0)
     grads(1, 1)
     grads(1, 2)
     f_relay(0)
     grads(1, 3)
+    f_fin1(0)
+    flip(1)
     out_sum()
-    dec_grads(0, 4)
+    dec_grads(0, 1)
     f_add(1)
+    dec_grads(1, 2)
     f_relay(1)
-    f_fin1(0)
-    dec_grads(4, 8)
     f_fin2(0)
     f_fin1(1)
+    dec_grads(2, 8)
     f_fin2(1)
 
-    for g in ax + [at] + ar[0] + ar[1]:
+    for g in ax + ar[0] + ar[1]:
+        if g is not ax[0]:
+            g.sent()
         g.drain()
     for r in range(CH):
         b_drain(r)
-        for n in range(NSTEPS):
-            remote(sibs.at[r, n], sibr.at[r, n], cs_s.at[r, n], cs_r.at[r, n], sib).wait_send()
+        remote(sibs.at[r], sibr.at[r], cs_s.at[r], cs_r.at[r, 0], sib).wait_send()
         for h in range(HALVES):
-            ref = ys.at[r, :, :, half(h)]
-            remote(ref, ref, cy_s.at[r, h], cy_r.at[r, h, 0], sib).wait_send()
-            z_copy(r, h).wait_send()
+            c_all(r, h).wait_send()
         for name in ("a1", "s1", "a2", "a3", "b2", "s2", "b3", "c3", "s3", "r0"):
 
             @pl.when(x == int(name[1]))
@@ -646,8 +559,7 @@
                     cp.wait_send()
 
         f_zcopy(r).wait_send()
-    for k in range(1, LAYERS):
-        norm_copy(k).wait_send()
+    norm_all().wait_send()
 
 
 def run_main(x, tgt, order, we, eb, w, db):
@@ -666,7 +578,7 @@
         in_specs=[any_spec, any_spec, vmem, any_spec, vmem, any_spec, vmem],
         out_specs=(vmem,) * 5,
         scratch_shapes=[
-            pltpu.VMEM((TOKS, 2 * PR, D), BF16),
+            pltpu.VMEM((128, D), BF16),
             pltpu.VMEM((CH, TOKS, PR, D), BF16),
             pltpu.VMEM((CH, CR, D), BF16),
             pltpu.VMEM((CH, CR, FS), BF16),
@@ -677,12 +589,9 @@
             pltpu.VMEM((CH, NSTEPS, 128, NT), F32),
             pltpu.VMEM((CH, NSTEPS, 128, NT), BF16),
             pltpu.VMEM((CH, NSTEPS, 128, NT), BF16),
-            pltpu.VMEM((CH, 6, PR, D), BF16),
-            pltpu.VMEM((CH, 6, PR, D), BF16),
-            pltpu.VMEM((CH, PR, D), BF16),
-            pltpu.VMEM((CH, PR, D), BF16),
-            pltpu.VMEM((CH, PR, D), F32),
-            pltpu.VMEM((CH, PR, D), F32),
+            pltpu.VMEM((CH, 8, PR, D), BF16),
+            pltpu.VMEM((CH, 8, PR, D), BF16),
+            pltpu.VMEM((CH, CR, 128), BF16),
             pltpu.VMEM((CH, LAYERS, CR, FS), BF16),
             pltpu.VMEM((CH, 2, CR, FS), F32),
             pltpu.VMEM((CH, 5, CR, FS), BF16),
@@ -691,11 +600,11 @@
             pltpu.VMEM((LAYERS, LAYERS, FS), F32),
             pltpu.VMEM((LAYERS, FS), F32),
             pltpu.VMEM((LAYERS, FS, ROWS), BF16),
-            dma((4 + LAYERS,)), dma((3 + CH * HALVES,)), dma((3 + CH * HALVES, TOKS)),
-            dma((CH, 9)), dma((CH, 10)), dma((CH, NSTEPS)), dma((CH, NSTEPS)),
-            dma((CH, HALVES)), dma((CH, HALVES, 6)), dma((CH, HALVES)), dma((CH, HALVES)),
+            dma((4 + LAYERS,)), dma((CH + CH * HALVES, 2)), dma((CH + CH * HALVES, 2)),
+            dma((CH, 9)), dma((CH, 10)), dma((CH,)), dma((CH, HALVES)),
+            dma((CH, HALVES)), dma((CH, HALVES)),
             dma((CH, 8)), dma((CH, 5)), dma((CH,)), dma((CH,)),
-            dma((LAYERS,)), dma((LAYERS,)),
+            dma((1,)), dma((1,)),
         ],
         compiler_params=pltpu.CompilerParams(
             collective_id=0, has_side_effects=True, vmem_limit_bytes=46 << 20
@@ -706,9 +615,11 @@
 
 def tail_kernel(x_ref, g_ref, d_ref, f_ref, o_ref, dw_hbm, dwe_hbm, fg_hbm, og_hbm, enc, sems):
     copies = [
-        pltpu.make_async_copy(d_ref, dw_hbm.at[0], sems.at[0]),
-        pltpu.make_async_copy(f_ref, fg_hbm, sems.at[2]),
-        pltpu.make_async_copy(o_ref, og_hbm, sems.at[3]),
+        pltpu.make_async_copy(d_ref.at[l], dw_hbm.at[0, l], sems.at[l]) for l in range(LAYERS)
+    ]
+    copies += [
+        pltpu.make_async_copy(f_ref, fg_hbm, sems.at[LAYERS]),
+        pltpu.make_async_copy(o_ref, og_hbm, sems.at[LAYERS + 1]),
     ]
     for cp in copies:
         cp.start()
@@ -717,7 +628,7 @@
         cs = slice(n * NT, (n + 1) * NT)
         part = jnp.dot(g, x_ref[:, :, :, cs].reshape(ROWS, NT), preferred_element_type=F32)
         enc[cs, :] = part.astype(BF16).T
-    copies.append(pltpu.make_async_copy(enc, dwe_hbm.at[0], sems.at[1]))
+    copies.append(pltpu.make_async_copy(enc, dwe_hbm.at[0], sems.at[LAYERS + 2]))
     copies[-1].start()
     for cp in copies:
         cp.wait()
@@ -736,7 +647,7 @@
         ),
         in_specs=[vmem] * 5,
         out_specs=(any_spec,) * 4,
-        scratch_shapes=[pltpu.VMEM((D, FS), BF16), pltpu.SemaphoreType.DMA((4,))],
+        scratch_shapes=[pltpu.VMEM((D, FS), BF16), pltpu.SemaphoreType.DMA((LAYERS + 3,))],
         compiler_params=pltpu.CompilerParams(vmem_limit_bytes=20 << 20),
         name="weights",
     )(xs, gl, dec, fg, og)

time: 102 us -> 89.6 us (0.88)
  Pallas kernels: 101 us -> 88.2 us
    pallas_call x1, Pallas kernels: 97 us -> 84.5 us  [run_main(): pl.pallas_call(main_kernel, out_shape=(pltpu.VMEM((CH, TOKS, PR, D), BF16...]
where the time goes in v3:
time: 89.6 us; the launch traced here: 89 us
  Pallas kernels  88.2 us (98%)
    pallas_call x1, Pallas kernels, run_main(): pl.pallas_call(main_kernel, out_shape=(pltpu.VMEM((CH, TOKS, PR, D), BF16...  84.5 us
    pallas_call x1, Pallas kernels, run_tail(): pl.pallas_call(tail_kernel, out_shape=(jax.ShapeDtypeStruct((1, LAYERS, F...  3.72 us

profile of v3, /device:TPU:1, one launch (start us, length us, event | category | flops | bytes accessed | tf_op | source)
XLA Modules:
  0.0 89.0 jit_solution(5190481567299504924)
XLA Ops:
  0.6 84.5 %window.1 = (bf16[2,16,16,2048]{3,2,1,0:T(8,128)(2,1)S(1)}, bf16[2,256,256]{2,1,0:T(8,128)(2,1)S(1)}, bf16[8,256,2048]{2,1,0:T(8,128)(2,1)S(1)}, f32[1,256]{1,0:T(1,128)S(1)}, f32[1,2048]{1,0:T(1,128)S(1)}) custom-call(bf16[1,32,2048]{2,1,0:T(8,128)(2,1)} %x_hbm.1, bf16[1,32,2048]{2,1,0:T(8,128)(2,1)} %t_hbm.1, s32[1,512]{1,0:T(1,128)} %bitcast.1, ...), custom_call_target="tpu_custom_call" | custom-call | tf_op jit(solution)/shard_map/window/pallas_call | solution.py:569
  85.1 3.7 %weights.1 = (bf16[1,8,256,2048]{3,2,1,0:T(8,128)(2,1)}, bf16[1,2048,256]{2,1,0:T(8,128)(2,1)}, f32[1,256]{1,0:T(1,128)}, f32[1,2048]{1,0:T(1,128)}) custom-call(bf16[2,16,16,2048]{3,2,1,0:T(8,128)(2,1)S(1)} %get-tuple-element.13.x_ref, bf16[2,256,256]{2,1,0:T(8,128)(2,1)S(1)} %get-tuple-element.14.g_ref, bf16[8,256,2048]{2,1,0:T(8,128)(2,1)S(1)} %get-tuple-element.15.d_ref, ...), custom_call_target="tpu_custom_call" | custom-call | tf_op jit(solution)/shard_map/weights/pallas_call | solution.py:640

commit v4 on v3

--- a/solution.py
+++ b/solution.py
@@ -330,20 +330,23 @@
         remote(frecv.at[r, slot], frecv.at[r, slot], f_s.at[r, 0], f_r.at[r, slot], sib).wait_recv()
 
     def f_sends(r, name):
+        def to_owner(l, base):
+            return f_copy(r, l, gb.at[r, l], base + zl, (l, t))
+
         return {
-            "a1": lambda: [f_copy(r, 0, gb.at[r, 0], 0, xdn)],
-            "s1": lambda: [f_copy(r, 1, gb.at[r, 1], 1, xdn)],
+            "a1": lambda: [to_owner(0, 0)],
+            "s1": lambda: [to_owner(1, 0)],
             "a2": lambda: [
                 f_copy(r, 0, gb.at[r, 0], 2, xup),
                 f_copy(r, 1, gb.at[r, 1], 4, xdn),
             ],
             "a3": lambda: [f_copy(r, 3, gb.at[r, 3], 4, xup), f_copy(r, 2, gb.at[r, 2], 4, xdn)],
-            "b2": lambda: [f_copy(r, 3, gb.at[r, 3], 1, xdn)],
-            "s2": lambda: [f_copy(r, 2, gb.at[r, 2], 0, xdn)],
-            "b3": lambda: [f_copy(r, 4 + l, gb.at[r, 4 + l], l, xdn) for l in (0, 1)],
-            "c3": lambda: [f_copy(r, 1, gb.at[r, 1], 3, xup)],
-            "s3": lambda: [f_copy(r, 0, gb.at[r, 0], 2, xup)],
-            "r0": lambda: [f_copy(r, 7, frecv.at[r, 4], 2, xup)],
+            "b2": lambda: [to_owner(3, 0)],
+            "s2": lambda: [to_owner(2, 0)],
+            "b3": lambda: [to_owner(4, 0), to_owner(5, 0)],
+            "c3": lambda: [to_owner(1, 2)],
+            "s3": lambda: [to_owner(0, 2)],
+            "r0": lambda: [f_copy(r, 7, frecv.at[r, 4], 2 + zl, (3, t))],
         }[name]()
 
     def f_go(r, name, before=None):
@@ -408,27 +411,30 @@
     def f_zcopy(r):
         return remote(fzs.at[r], fzr.at[r], fz_s.at[r], fz_r.at[r], zpl)
 
-    def f_fin1(r):
-        for cond, adds in (
-            (x == 0, ((0, 0), (1, 1), (0, 2), (1, 3))),
-            (x == 1, ((0, 0), (1, 1), (1, 2))),
-            (x == 2, ((0, 0), (1, 1))),
-        ):
+    def f_own(r):
+        @pl.when(zl == 1)
+        def _():
+            fzs[r] = gown[r, 0].astype(BF16)
+            f_zcopy(r).start()
+
+    def f_fin(r):
+        gown[r, 0] = jnp.where(zl == 1, gown[r, 1], gown[r, 0])
+
+        @pl.when(zl == 0)
+        def _():
+            f_zcopy(r).wait_recv()
+            gown[r, 0] = gown[r, 0] + fzr[r].astype(F32)
+
+        for cond, slots in ((x < 3, (0, 1)), ((x == 0) | (m == 3), (2, 3))):
 
             @pl.when(cond)
-            def _(adds=adds):
-                for j, slot in adds:
+            def _(slots=slots):
+                for slot in slots:
                     f_wait(r, slot)
-                    gown[r, j] = gown[r, j] + frecv[r, slot].astype(F32)
-
-        fzs[r] = gown[r, 1 - zl].astype(BF16)
-        f_zcopy(r).start()
-
-    def f_fin2(r):
-        remote(fzr.at[r], fzr.at[r], fz_s.at[r], fz_r.at[r], sib).wait_recv()
-        total = gown[r, zl] + fzr[r].astype(F32)
+                    gown[r, 0] = gown[r, 0] + frecv[r, slot].astype(F32)
+
         norm = no_ref[pl.ds(m, 1), :]
-        grad = jnp.where(pre[r] > 0, total + norm * SCALE, 0.0)
+        grad = jnp.where(pre[r] > 0, gown[r, 0] + norm * SCALE, 0.0)
         go[r] = grad.astype(BF16)
         fsum = jnp.sum(grad, axis=0, keepdims=True)
         fo[...] = fsum if r == 0 else fo[...] + fsum
@@ -518,6 +524,7 @@
     grads(0, 1)
     grads(0, 2)
     grads(0, 3)
+    f_own(0)
     ar[1][0].take()
     ar[1][1].take()
     f_add(0)
@@ -530,17 +537,16 @@
     grads(1, 2)
     f_relay(0)
     grads(1, 3)
-    f_fin1(0)
+    f_own(1)
     flip(1)
     out_sum()
     dec_grads(0, 1)
     f_add(1)
     dec_grads(1, 2)
     f_relay(1)
-    f_fin2(0)
-    f_fin1(1)
+    f_fin(0)
     dec_grads(2, 8)
-    f_fin2(1)
+    f_fin(1)
 
     for g in ax + ar[0] + ar[1]:
         if g is not ax[0]:
@@ -558,7 +564,7 @@
                 for cp in f_sends(r, name):
                     cp.wait_send()
 
-        f_zcopy(r).wait_send()
+        pl.when(zl == 1)(f_zcopy(r).wait_send)
     norm_all().wait_send()
 
 

time: 89.6 us -> 86.1 us (0.961)
  Pallas kernels: 88.2 us -> 85.2 us
    pallas_call x1, Pallas kernels: 84.5 us -> 81.5 us  [run_main(): pl.pallas_call(main_kernel, out_shape=(pltpu.VMEM((CH, TOKS, PR, D), BF16...]
where the time goes in v4:
time: 86.1 us; the launch traced here: 86 us
  Pallas kernels  85.2 us (99%)
    pallas_call x1, Pallas kernels, run_main(): pl.pallas_call(main_kernel, out_shape=(pltpu.VMEM((CH, TOKS, PR, D), BF16...  81.5 us
    pallas_call x1, Pallas kernels, run_tail(): pl.pallas_call(tail_kernel, out_shape=(jax.ShapeDtypeStruct((1, LAYERS, F...  3.72 us

profile of v4, /device:TPU:1, one launch (start us, length us, event | category | flops | bytes accessed | tf_op | source)
XLA Modules:
  0.0 86.0 jit_solution(17240148841861699411)
XLA Ops:
  0.6 81.5 %window.1 = (bf16[2,16,16,2048]{3,2,1,0:T(8,128)(2,1)S(1)}, bf16[2,256,256]{2,1,0:T(8,128)(2,1)S(1)}, bf16[8,256,2048]{2,1,0:T(8,128)(2,1)S(1)}, f32[1,256]{1,0:T(1,128)S(1)}, f32[1,2048]{1,0:T(1,128)S(1)}) custom-call(bf16[1,32,2048]{2,1,0:T(8,128)(2,1)} %x_hbm.1, bf16[1,32,2048]{2,1,0:T(8,128)(2,1)} %t_hbm.1, s32[1,512]{1,0:T(1,128)} %bitcast.1, ...), custom_call_target="tpu_custom_call" | custom-call | tf_op jit(solution)/shard_map/window/pallas_call | solution.py:575
  82.1 3.7 %weights.1 = (bf16[1,8,256,2048]{3,2,1,0:T(8,128)(2,1)}, bf16[1,2048,256]{2,1,0:T(8,128)(2,1)}, f32[1,256]{1,0:T(1,128)}, f32[1,2048]{1,0:T(1,128)}) custom-call(bf16[2,16,16,2048]{3,2,1,0:T(8,128)(2,1)S(1)} %get-tuple-element.13.x_ref, bf16[2,256,256]{2,1,0:T(8,128)(2,1)S(1)} %get-tuple-element.14.g_ref, bf16[8,256,2048]{2,1,0:T(8,128)(2,1)S(1)} %get-tuple-element.15.d_ref, ...), custom_call_target="tpu_custom_call" | custom-call | tf_op jit(solution)/shard_map/weights/pallas_call | solution.py:646

commit v5 on v4

--- a/solution.py
+++ b/solution.py
@@ -517,10 +517,10 @@
     ar[0][0].take()
     ar[0][1].take()
     c_d(1, 0)
-    c_d(1, 1)
     ar[0][0].finish()
     ar[0][1].finish()
     grads(0, 0)
+    c_d(1, 1)
     grads(0, 1)
     grads(0, 2)
     grads(0, 3)

time: 86.1 us -> 85.9 us (level)
  no operation moved by 1% of the time
where the time goes in v5:
time: 85.9 us; the launch traced here: 85.8 us
  Pallas kernels  85 us (99%)
    pallas_call x1, Pallas kernels, run_main(): pl.pallas_call(main_kernel, out_shape=(pltpu.VMEM((CH, TOKS, PR, D), BF16...  81.3 us
    pallas_call x1, Pallas kernels, run_tail(): pl.pallas_call(tail_kernel, out_shape=(jax.ShapeDtypeStruct((1, LAYERS, F...  3.72 us

profile of v5, /device:TPU:1, one launch (start us, length us, event | category | flops | bytes accessed | tf_op | source)
XLA Modules:
  0.0 85.8 jit_solution(10116087306213308096)
XLA Ops:
  0.6 81.3 %window.1 = (bf16[2,16,16,2048]{3,2,1,0:T(8,128)(2,1)S(1)}, bf16[2,256,256]{2,1,0:T(8,128)(2,1)S(1)}, bf16[8,256,2048]{2,1,0:T(8,128)(2,1)S(1)}, f32[1,256]{1,0:T(1,128)S(1)}, f32[1,2048]{1,0:T(1,128)S(1)}) custom-call(bf16[1,32,2048]{2,1,0:T(8,128)(2,1)} %x_hbm.1, bf16[1,32,2048]{2,1,0:T(8,128)(2,1)} %t_hbm.1, s32[1,512]{1,0:T(1,128)} %bitcast.1, ...), custom_call_target="tpu_custom_call" | custom-call | tf_op jit(solution)/shard_map/window/pallas_call | solution.py:575
  81.9 3.7 %weights.1 = (bf16[1,8,256,2048]{3,2,1,0:T(8,128)(2,1)}, bf16[1,2048,256]{2,1,0:T(8,128)(2,1)}, f32[1,256]{1,0:T(1,128)}, f32[1,2048]{1,0:T(1,128)}) custom-call(bf16[2,16,16,2048]{3,2,1,0:T(8,128)(2,1)S(1)} %get-tuple-element.13.x_ref, bf16[2,256,256]{2,1,0:T(8,128)(2,1)S(1)} %get-tuple-element.14.g_ref, bf16[8,256,2048]{2,1,0:T(8,128)(2,1)S(1)} %get-tuple-element.15.d_ref, ...), custom_call_target="tpu_custom_call" | custom-call | tf_op jit(solution)/shard_map/weights/pallas_call | solution.py:646
